TPU v7x, 256 devices: a whole 4x4x8 slice. The times are simulated.
256 devices in a mesh: node: 4 (over x), table: 64 (over y, z, core).
Axes of the slice: x: 4, y: 4, z: 8, core: 2. Of those that a mesh axis runs over, the one named last changes fastest.
Arguments:
- emb_rows: bfloat16 [131072, 128], P(('node', 'table')), may hold values from -0.23925781 to 0.23925781
- tile_mult: int32 [16384, 128, 128], P(('node', 'table')), may hold values from 0 to 3
- tile_rows: int32 [16384], P(('node', 'table')), may hold values from 0 to 3
- tile_table: int32 [16384], P(('node', 'table')), may hold values from 0 to 63, as said below
- tile_slot: int32 [16384], P(('node', 'table')), may hold values from 0 to 51
- dense: bfloat16 [65536, 128], P(('node', 'table')), may hold values from -6 to 6
- cross_v: bfloat16 [3456, 512], P('node'), may hold values from -0.109375 to 0.109375
- cross_u: bfloat16 [512, 3456], P('node'), may hold values from -0.25 to 0.25
- cross_bias: float32 [3456], replicated, may hold values from -3 to 3
- cotangent: bfloat16 [65536, 3456], P(('node', 'table')), may hold values from -0.1796875 to 0.1796875
Outputs:
- cross_out: bfloat16 [65536, 3456], P(('node', 'table'))
- emb_grad: float32 [131072, 128], P(('node', 'table'))
Inputs may be any that keep to these rules, and one draw needn't show every extreme that they name: For each node index n and table index t, take the tiles j with j // 16 == n on the 4 devices of table index t: no tile_table value occurs more than 3 times among them, and the tiles with one value carry at most 2 distinct tile_slot values. Both bounds are reached in every such set.
All inputs are finite; a program needn't handle non-finite values.
Results may differ from a plain program's by a relative error of at most 0.0057.
Values may be sent and summed in bfloat16 or wider, within the bound.
A program may use at most 128 MiB of HBM per device.

v0:
```python
import jax
import jax.numpy as jnp
from jax import lax
from jax.sharding import PartitionSpec as P

FEATURES = 26
CAP = 3
SAMPLE_BLOCKS = 2
BAG_BLOCKS = 52


def place(flat_values, slot_ids, list_entry, member_rank, entries):
    sequence = jnp.arange(slot_ids.shape[0], dtype=jnp.int32)
    targets = jnp.arange(entries, dtype=jnp.int32)[:, None]
    chosen = (list_entry[None, :] == targets) & (member_rank[None, :] == 0)
    present = jnp.any(chosen, axis=1)
    source = jnp.sum(jnp.where(chosen, sequence[None, :], 0), axis=1)
    filled = jnp.where(present[:, None], jnp.take(flat_values, source, axis=0), 0.0)
    first_slot = jnp.where(present, jnp.take(slot_ids, source), -1).astype(jnp.int32)
    return (filled, first_slot)


def owner_work(arrived, arrived_slot, dense, cross_v, cross_u, cross_bias, cotangent):
    block_size = arrived.shape[2]
    emb_width = arrived.shape[3]
    flat_arrived = arrived.reshape(-1, block_size * emb_width)
    flat_slot = arrived_slot.reshape(-1)
    selector = (flat_slot[None, :] == jnp.arange(BAG_BLOCKS, dtype=jnp.int32)[:, None]).astype(
        jnp.float32
    )
    pooled = jnp.dot(
        selector, flat_arrived, precision=lax.Precision.HIGHEST, preferred_element_type=jnp.float32
    )
    embedded = pooled.reshape(FEATURES, SAMPLE_BLOCKS, block_size, emb_width).transpose(1, 2, 0, 3)
    embedded = embedded.reshape(-1, FEATURES * emb_width).astype(jnp.bfloat16)
    first_layer = jnp.concatenate([dense, embedded], axis=1)
    hidden = jnp.dot(first_layer, cross_v, preferred_element_type=jnp.float32).astype(jnp.bfloat16)
    cross_scale = jnp.dot(hidden, cross_u, preferred_element_type=jnp.float32) + cross_bias
    layer_input = first_layer.astype(jnp.float32)
    cross_out = (layer_input * (cross_scale + 1.0)).astype(jnp.bfloat16)
    upstream = cotangent.astype(jnp.float32)
    dscale = (upstream * layer_input).astype(jnp.bfloat16)
    dhidden = lax.dot_general(
        dscale, cross_u, (((1,), (1,)), ((), ())), preferred_element_type=jnp.float32
    ).astype(jnp.bfloat16)
    dlayer = upstream * (cross_scale + 1.0) + lax.dot_general(
        dhidden, cross_v, (((1,), (1,)), ((), ())), preferred_element_type=jnp.float32
    )
    bag_grad = (
        dlayer[:, emb_width:]
        .astype(jnp.bfloat16)
        .reshape(SAMPLE_BLOCKS, block_size, FEATURES, emb_width)
    )
    bag_grad = bag_grad.transpose(2, 0, 1, 3).reshape(BAG_BLOCKS, block_size, emb_width)
    occupied = arrived_slot >= 0
    safe_slot = jnp.where(occupied, arrived_slot, 0)
    returning = jnp.where(
        occupied[..., None, None],
        jnp.take(bag_grad, safe_slot, axis=0),
        jnp.zeros((), jnp.bfloat16),
    )
    return (cross_out, returning)


def body(
    emb_rows,
    tile_mult,
    tile_rows,
    tile_table,
    tile_slot,
    dense,
    cross_v,
    cross_u,
    cross_bias,
    cotangent,
):
    tables = lax.axis_size("table")
    tile_count = tile_mult.shape[0]
    block_size = tile_mult.shape[1]
    emb_width = emb_rows.shape[1]
    row_blocks = emb_rows.reshape(-1, block_size, emb_width)
    tile_weights = tile_mult.astype(jnp.bfloat16)
    picked = jnp.take(row_blocks, tile_rows, axis=0)
    partial_rows = jnp.einsum(
        "kbr,kre->kbe", tile_weights, picked, preferred_element_type=jnp.float32
    )
    forwarded, moved_table, moved_slot = (
        lax.all_to_all(partial_rows, "node", split_axis=0, concat_axis=0, tiled=True),
        lax.all_to_all(tile_table, "node", split_axis=0, concat_axis=0, tiled=True),
        lax.all_to_all(tile_slot, "node", split_axis=0, concat_axis=0, tiled=True),
    )
    full_v, full_u = (
        lax.all_gather(cross_v, "node", axis=0, tiled=True),
        lax.all_gather(cross_u, "node", axis=0, tiled=True),
    )
    sequence = jnp.arange(tile_count, dtype=jnp.int32)
    earlier = sequence[None, :] < sequence[:, None]
    same_table = moved_table[:, None] == moved_table[None, :]
    flat_moved = forwarded.reshape(tile_count, -1)
    list_depth = CAP
    list_rank = jnp.sum(same_table & earlier, axis=1)
    list_entry = moved_table * list_depth + list_rank
    send_rows, send_slot = place(
        flat_moved, moved_slot, list_entry, jnp.zeros_like(list_entry), tables * list_depth
    )
    arrived, arrived_slot = (
        lax.all_to_all(
            send_rows.reshape(tables, list_depth, block_size, emb_width),
            "table",
            split_axis=0,
            concat_axis=0,
            tiled=True,
        ),
        lax.all_to_all(
            send_slot.reshape(tables, list_depth), "table", split_axis=0, concat_axis=0, tiled=True
        ),
    )
    cross_out, returning = owner_work(
        arrived, arrived_slot, dense, full_v, full_u, cross_bias, cotangent
    )
    came_back = lax.all_to_all(returning, "table", split_axis=0, concat_axis=0, tiled=True)
    tile_grad = jnp.take(
        came_back.reshape(tables * list_depth, block_size, emb_width), list_entry, axis=0
    )
    tile_grad = lax.all_to_all(tile_grad, "node", split_axis=0, concat_axis=0, tiled=True)
    tile_grads = jnp.einsum(
        "kbr,kbe->kre", tile_weights, tile_grad, preferred_element_type=jnp.float32
    )
    owner_rows = (
        tile_rows[None, :] == jnp.arange(row_blocks.shape[0], dtype=jnp.int32)[:, None]
    ).astype(jnp.float32)
    emb_grad = jnp.dot(
        owner_rows,
        tile_grads.reshape(tile_count, -1),
        precision=lax.Precision.HIGHEST,
        preferred_element_type=jnp.float32,
    )
    return (cross_out, emb_grad.reshape(-1, emb_width))


def solution(mesh):
    in_specs = (
        P(("node", "table"), None),
        P(("node", "table"), None, None),
        P(("node", "table")),
        P(("node", "table")),
        P(("node", "table")),
        P(("node", "table"), None),
        P("node", None),
        P("node", None),
        P(),
        P(("node", "table"), None),
    )
    out_specs = (P(("node", "table"), None), P(("node", "table"), None))
    return jax.shard_map(body, mesh=mesh, in_specs=in_specs, out_specs=out_specs, check_vma=False)
```

profile of v0, /device:TPU:1, one launch (start us, length us, event | category | flops | bytes accessed | tf_op | source)
XLA Modules:
  0.0 717.6 jit_solution(14621087533226989422)
XLA Ops:
  7.2 1.4 all_to_all.36
  8.5 4.8 all-to-all-start
  13.4 0.7 compare_select_fusion.8
  14.0 1.3 all_to_all.39
  15.3 2.1 all-to-all-done
  17.4 3.2 all-to-all-start.1
  20.6 0.5 broadcast.229
  21.2 0.7 multiply_reduce_fusion
  21.8 0.1 all_to_all.38
  21.9 0.2 convert_reduce_fusion
  22.1 0.1 select_reduce_fusion
  22.2 0.1 fusion.25
  22.3 0.1 reduce_sum.28
  22.5 2.2 all-to-all-done.1
  24.6 0.7 reduce.14
  25.3 0.1 all_to_all.41
  25.4 1.6 gather_fusion
  26.9 0.1 gather.25
  27.1 0.2 reduce_or.12
  27.2 0.6 select_select_fusion.2
  27.9 14.9 %all-to-all-start.2 = ((s32[64,1,3]{2,1,0:T(1,128)}), s32[64,1,3]{2,1,0:T(1,128)S(1)}, u32[]{:S(2)}, u32[]{:S(2)}) async-start(s32[64,1,3]{2,1,0:T(1,128)} %bitcast.4), calls=%async_computation.2 | async-start | bytes 65536 | tf_op jit(solution)/shard_map/all_to_all | solution.py:114
  42.8 0.7 compare_and_fusion.3
  43.4 8.5 %all-to-all-done.2 = s32[64,1,3]{2,1,0:T(1,128)S(1)} async-done(((s32[64,1,3]{2,1,0:T(1,128)}), s32[64,1,3]{2,1,0:T(1,128)S(1)}, u32[]{:S(2)}, u32[]{:S(2)}) %all-to-all-start.2) | async-done | bytes 800 | tf_op jit(solution)/shard_map/all_to_all | solution.py:114
  52.0 0.1 reshape.277
  52.2 1.0 gather_fusion.1
  53.1 2.9 copy.36
  56.0 6.4 convolution_bitcast_fusion.1
  62.4 4.8 all-to-all-start.3
  67.3 0.1 reduce_sum.30
  67.4 0.2 broadcast_in_dim.107
  67.6 48.0 %all-to-all-done.3 = f32[64,128,128]{1,2,0:T(8,128)} async-done(((f32[64,128,128]{1,2,0:T(8,128)}), f32[64,128,128]{1,2,0:T(8,128)}, u32[]{:S(2)}, u32[]{:S(2)}) %all-to-all-start.3) | async-done | bytes 4194336 | tf_op jit(solution)/shard_map/all_to_all | solution.py:88
  115.5 6.1 copy.37
  121.7 6.5 copy.68
  128.2 16.1 %gather_fusion.2 = f32[192,16384]{1,0:T(8,128)} fusion(f32[64,16384]{1,0:T(8,128)} %bitcast.77, s32[1024]{0:T(1024)S(1)} %pad_clamp_fusion.3), kind=kCustom, calls=%fused_computation.2 | custom fusion | bytes 25166592 | tf_op jit(solution)/shard_map/jit(_take)/gather | solution.py:18
  144.3 11.6 %copy.49 = f32[24,8,128,128]{3,2,1,0:T(8,128)} copy(f32[24,8,128,128]{3,1,2,0:T(8,128)} %bitcast.79) | data formatting | bytes 25165824
  155.8 10.5 %select_select_fusion = f32[64,3,128,128]{3,2,1,0:T(8,128)} fusion(f32[64,3,128,128]{3,2,1,0:T(8,128)} %bitcast.78, pred[64,3]{1,0:T(8,128)(4,1)S(1)} %compare_and_fusion.1, pred[64,3]{1,0:T(8,128)(4,1)S(1)} %broadcast_in_dim.107), kind=kLoop, calls=%fused_computation.9 | loop fusion | flops 6291456 | bytes 25166208 | tf_op jit(solution)/shard_map/jit(_where)/select_n | solution.py:18
  166.3 6.8 all-to-all-start.4
  173.2 0.7 all-gather.3.cloned.1.call-update
  174.0 0.7 all-gather.5.cloned.1.call-update
  174.7 2.0 convert_element_type.44
  176.7 0.6 constant_dynamic-update-slice_fusion
  177.3 0.7 reduce.15
  178.1 0.1 eq.71
  178.2 270.7 %all-to-all-done.4 = f32[64,3,128,128]{3,2,1,0:T(8,128)} async-done(((f32[64,3,128,128]{3,2,1,0:T(8,128)}), f32[64,3,128,128]{3,2,1,0:T(8,128)}, u32[]{:S(2)}, u32[]{:S(2)}) %all-to-all-start.4) | async-done | bytes 12582944 | tf_op jit(solution)/shard_map/all_to_all | solution.py:107
  448.9 16.6 %fusion.11 = bf16[26,2,128,128]{3,0,2,1:T(8,128)(2,1)S(1)} fusion(s32[26,2]{0,1:T(2,128)S(1)} %multiply_add_fusion, s32[192]{0:T(256)S(1)} %eq.71, f32[24,8,128,128]{3,2,1,0:T(8,128)} %bitcast.30), kind=kOutput, calls=%fused_computation.29 | convolution fusion | flops 1963796224 | bytes 14287824 | tf_op jit(solution)/shard_map/dot_general | solution.py:31
  465.5 2.0 bitcast_dynamic-update-slice_fusion
  467.5 7.6 %fusion.21 = f32[256,3456]{1,0:T(8,128)} fusion(bf16[3456,512]{1,0:T(8,128)(2,1)} %all-gather.3.cloned.1.call-done, bf16[512,3456]{1,0:T(8,128)(2,1)} %all-gather.5.cloned.1.call-done, bf16[256,3456]{1,0:T(8,128)(2,1)} %bitcast_dynamic-update-slice_fusion, bf16[256,3456]{1,0:T(8,128)(2,1)S(1)} %copy-done.3), kind=kOutput, calls=%fused_computation.37 | convolution fusion | flops 1815609344 | bytes 14155776 | tf_op jit(solution)/shard_map/dot_general | solution.py:46
  475.1 8.7 %fusion.6 = (bf16[256,3456]{1,0:T(8,128)(2,1)}, f32[256,3456]{1,0:T(8,128)}) fusion(bf16[256,3456]{1,0:T(8,128)(2,1)} %bitcast_dynamic-update-slice_fusion, f32[3456]{0:T(1024)S(1)} %copy-done.6, bf16[512,3456]{1,0:T(8,128)(2,1)} %all-gather.5.cloned.1.call-done, bf16[3456,512]{1,0:T(8,128)(2,1)} %all-gather.3.cloned.1.call-done), kind=kOutput, calls=%fused_computation.19 | convolution fusion | flops 1816494080 | bytes 14169600 | tf_op jit(solution)/shard_map/dot_general | solution.py:38
  483.8 4.4 fusion.8
  488.2 1.3 copy.41
  489.5 1.4 reshape.246
  491.0 4.6 copy.42
  495.6 8.0 %gather_fusion.3 = bf16[192,128,128]{2,1,0:T(8,128)(2,1)} fusion(bf16[52,128,128]{2,1,0:T(8,128)(2,1)S(1)} %bitcast.80, s32[1024]{0:T(1024)S(1)} %get-tuple-element.10), kind=kCustom, calls=%fused_computation.3 | custom fusion | bytes 12583680 | tf_op jit(solution)/shard_map/jit(_take)/gather | solution.py:59
  503.5 6.8 select_select_fusion.1
  510.3 6.2 all-to-all-start.5
  516.6 140.8 %all-to-all-done.5 = bf16[64,3,128,128]{3,2,1,0:T(8,128)(2,1)} async-done(((bf16[64,3,128,128]{3,2,1,0:T(8,128)(2,1)}), bf16[64,3,128,128]{3,2,1,0:T(8,128)(2,1)}, u32[]{:S(2)}, u32[]{:S(2)}) %all-to-all-start.5) | async-done | bytes 6291488 | tf_op jit(solution)/shard_map/all_to_all | solution.py:121
  657.3 4.9 gather_fusion.4
  662.3 3.2 copy.43
  665.5 0.3 broadcast_select_fusion
  665.8 29.5 %all_to_all.56 = bf16[64,128,128]{1,2,0:T(8,128)(2,1)S(1)} all-to-all(bf16[64,128,128]{1,2,0:T(8,128)(2,1)S(1)} %broadcast_select_fusion), channel_id=1, replica_groups=mesh['node'=4,'table'=64] {'node'}, dimensions={0} | all-to-all | bytes 4194304 | tf_op jit(solution)/shard_map/all_to_all | solution.py:125
  695.3 2.7 convolution_bitcast_fusion
  698.0 5.7 copy.44
  703.7 5.8 fusion.3
  709.4 0.9 reshape.250
  (29 shorter events, 0.3 us)
Async XLA Ops:
  7.2 45.0 %copy-start = (bf16[512,128]{1,0:T(8,128)(2,1)S(1)}, bf16[512,128]{1,0:T(8,128)(2,1)}, u32[]{:S(2)}) copy-start(bf16[512,128]{1,0:T(8,128)(2,1)} %param.10) | copy-start | bytes 393220
  8.5 8.9 %all-to-all-start = ((s32[4,16,1]{1,2,0:T(1,128)}), s32[4,16,1]{1,2,0:T(1,128)S(1)}, u32[]{:S(2)}, u32[]{:S(2)}) async-start(s32[4,16,1]{1,2,0:T(1,128)} %bitcast), calls=%async_computation | async-start | bytes 4096 | tf_op jit(solution)/shard_map/all_to_all | solution.py:89
  17.4 7.2 %all-to-all-start.1 = ((s32[4,16,1]{1,2,0:T(1,128)}), s32[4,16,1]{1,2,0:T(1,128)S(1)}, u32[]{:S(2)}, u32[]{:S(2)}) async-start(s32[4,16,1]{1,2,0:T(1,128)} %bitcast.1), calls=%async_computation.1 | async-start | bytes 4096 | tf_op jit(solution)/shard_map/all_to_all | solution.py:90
  27.9 24.1 %all-to-all-start.2 = ((s32[64,1,3]{2,1,0:T(1,128)}), s32[64,1,3]{2,1,0:T(1,128)S(1)}, u32[]{:S(2)}, u32[]{:S(2)}) async-start(s32[64,1,3]{2,1,0:T(1,128)} %bitcast.4), calls=%async_computation.2 | async-start | bytes 65536 | tf_op jit(solution)/shard_map/all_to_all | solution.py:114
  62.4 53.1 %all-to-all-start.3 = ((f32[64,128,128]{1,2,0:T(8,128)}), f32[64,128,128]{1,2,0:T(8,128)}, u32[]{:S(2)}, u32[]{:S(2)}) async-start(f32[64,128,128]{1,2,0:T(8,128)} %convolution_bitcast_fusion.1), calls=%async_computation.3 | async-start | bytes 8388608 | tf_op jit(solution)/shard_map/all_to_all | solution.py:88
  166.3 8.3 %copy-start.3 = (bf16[256,3456]{1,0:T(8,128)(2,1)S(1)}, bf16[256,3456]{1,0:T(8,128)(2,1)}, u32[]{:S(2)}) copy-start(bf16[256,3456]{1,0:T(8,128)(2,1)} %param.19) | copy-start | bytes 5308420
  166.3 282.5 %all-to-all-start.4 = ((f32[64,3,128,128]{3,2,1,0:T(8,128)}), f32[64,3,128,128]{3,2,1,0:T(8,128)}, u32[]{:S(2)}, u32[]{:S(2)}) async-start(f32[64,3,128,128]{3,2,1,0:T(8,128)} %select_select_fusion), calls=%async_computation.4 | async-start | bytes 25165824 | tf_op jit(solution)/shard_map/all_to_all | solution.py:107
  173.2 3.5 copy-start.4
  173.2 294.4 %all-gather.3.cloned.1.call-start = ((), (), s32[]{:S(2)}) async-start(), calls=%async_computation.7 | async-start | bytes 4423680 | tf_op jit(solution)/shard_map/all_gather | solution.py:93
  173.9 293.6 %all-gather.5.cloned.1.call-start = ((), (), s32[]{:S(2)}) async-start(), calls=%async_computation.8 | async-start | bytes 4423680 | tf_op jit(solution)/shard_map/all_gather | solution.py:94
  467.5 7.6 %copy-start.6 = (f32[3456]{0:T(1024)S(1)}, f32[3456]{0:T(1024)}, u32[]{:S(2)}) copy-start(f32[3456]{0:T(1024)} %param.18) | copy-start | bytes 41476
  510.3 147.0 %all-to-all-start.5 = ((bf16[64,3,128,128]{3,2,1,0:T(8,128)(2,1)}), bf16[64,3,128,128]{3,2,1,0:T(8,128)(2,1)}, u32[]{:S(2)}, u32[]{:S(2)}) async-start(bf16[64,3,128,128]{3,2,1,0:T(8,128)(2,1)} %select_select_fusion.1), calls=%async_computation.5 | async-start | bytes 12582912 | tf_op jit(solution)/shard_map/all_to_all | solution.py:121
  665.5 29.8 %copy-start.2 = (s32[64,128,128]{2,1,0:T(8,128)S(1)}, s32[64,128,128]{2,1,0:T(8,128)}, u32[]{:S(2)}) copy-start(s32[64,128,128]{2,1,0:T(8,128)} %param.11) | copy-start | bytes 12582916
  698.0 5.7 copy-start.5
  698.0 12.3 %copy-start.1 = (bf16[512,128]{1,0:T(8,128)(2,1)S(1)}, bf16[512,128]{1,0:T(8,128)(2,1)}, u32[]{:S(2)}) copy-start(bf16[512,128]{1,0:T(8,128)(2,1)} %param.10) | copy-start | bytes 393220
Sparse Core Ops, SparseCore 0:
  175.8 44.5 all-gather.2
  222.2 45.6 all-gather.4
where the time goes:
time: 723 us; the launch traced here: 718 us
  waiting for transfers between devices  474 us (66%)
  local copies, waits for them, and re-layouts  82.8 us (11%)
  matrix products  47.7 us (7%)
  starting transfers between devices  40.9 us (6%)
  blocking collectives  29.5 us (4%)
  other arithmetic  28.4 us (4%)
  between operations  14.7 us (2%)
    all_to_all x1, waiting for transfers between devices, body(): lax.all_to_all(send_rows.reshape(tables, list_depth, block_size, emb_widt...  271 us
    all_to_all x1, waiting for transfers between devices, body(): lax.all_to_all(returning, 'table', split_axis=0, concat_axis=0, tiled=True)  141 us
    all_to_all x1, waiting for transfers between devices, body(): lax.all_to_all(partial_rows, 'node', split_axis=0, concat_axis=0, tiled=T...  48 us
    all_to_all x1, blocking collectives, body(): lax.all_to_all(tile_grad, 'node', split_axis=0, concat_axis=0, tiled=True)  29.5 us
    unnamed x17, local copies, waits for them, and re-layouts  18.7 us
    dot_general x1, matrix products, owner_work(): jnp.dot(selector, flat_arrived, precision=lax.Precision.HIGHEST, preferre...  16.6 us
    gather x1, local copies, waits for them, and re-layouts, place(): jnp.take(flat_values, source, axis=0)  16.1 us
    all_to_all x1, starting transfers between devices, body(): lax.all_to_all(send_slot.reshape(tables, list_depth), 'table', split_axis...  14.9 us
  transfers between devices with their start and end apart: 8, of which 6 were waited for; matrix products, arithmetic and copies ran while one was open for 4% of the time, Pallas kernels for 0%

commit v1 on v0

v1 whole, which is shorter than its diff:
```python
import jax
import jax.numpy as jnp
from jax import lax
from jax.sharding import PartitionSpec as P

FEATURES = 26
DEPTH = 2
SAMPLE_BLOCKS = 2
BAG_BLOCKS = 52


def owner_work(arrived, arrived_slot, dense, cross_v, cross_u, cross_bias, cotangent):
    block_size = arrived.shape[-2]
    emb_width = arrived.shape[-1]
    flat_arrived = arrived.reshape(-1, block_size * emb_width)
    flat_slot = arrived_slot.reshape(-1)
    selector = flat_slot[None, :] == jnp.arange(BAG_BLOCKS, dtype=jnp.int32)[:, None]
    pooled = jnp.dot(
        selector.astype(jnp.bfloat16), flat_arrived, preferred_element_type=jnp.float32
    )
    embedded = pooled.reshape(FEATURES, SAMPLE_BLOCKS, block_size, emb_width).transpose(1, 2, 0, 3)
    embedded = embedded.reshape(-1, FEATURES * emb_width).astype(jnp.bfloat16)
    first_layer = jnp.concatenate([dense, embedded], axis=1)
    hidden = jnp.dot(first_layer, cross_v, preferred_element_type=jnp.float32).astype(jnp.bfloat16)
    cross_scale = jnp.dot(hidden, cross_u, preferred_element_type=jnp.float32) + cross_bias
    layer_input = first_layer.astype(jnp.float32)
    cross_out = (layer_input * (cross_scale + 1.0)).astype(jnp.bfloat16)
    upstream = cotangent.astype(jnp.float32)
    dscale = (upstream * layer_input).astype(jnp.bfloat16)
    dhidden = lax.dot_general(
        dscale, cross_u, (((1,), (1,)), ((), ())), preferred_element_type=jnp.float32
    ).astype(jnp.bfloat16)
    dlayer = upstream * (cross_scale + 1.0) + lax.dot_general(
        dhidden, cross_v, (((1,), (1,)), ((), ())), preferred_element_type=jnp.float32
    )
    bag_grad = (
        dlayer[:, emb_width:]
        .astype(jnp.bfloat16)
        .reshape(SAMPLE_BLOCKS, block_size, FEATURES, emb_width)
    )
    bag_grad = bag_grad.transpose(2, 0, 1, 3).reshape(BAG_BLOCKS, block_size * emb_width)
    returning = lax.dot_general(
        selector.astype(jnp.bfloat16), bag_grad, (((0,), (0,)), ((), ())),
        preferred_element_type=jnp.float32,
    ).astype(jnp.bfloat16)
    return cross_out, returning.reshape(arrived.shape)


def body(
    emb_rows,
    tile_mult,
    tile_rows,
    tile_table,
    tile_slot,
    dense,
    cross_v,
    cross_u,
    cross_bias,
    cotangent,
):
    tables = lax.axis_size("table")
    nodes = lax.axis_size("node")
    tile_count = tile_mult.shape[0]
    block_size = tile_mult.shape[1]
    emb_width = emb_rows.shape[1]
    local_blocks = emb_rows.shape[0] // block_size
    row_blocks = emb_rows.reshape(-1, block_size, emb_width)
    mult_bf = tile_mult.astype(jnp.bfloat16)

    meta = jnp.stack([tile_table, tile_slot, tile_rows], axis=1)
    moved_meta = lax.all_to_all(meta, "node", split_axis=0, concat_axis=0, tiled=True)
    moved_mult = lax.all_to_all(mult_bf, "node", split_axis=0, concat_axis=0, tiled=True)
    peer_rows = lax.all_gather(row_blocks, "node", axis=0, tiled=True)
    full_v = lax.all_gather(cross_v, "node", axis=0, tiled=True)
    full_u = lax.all_gather(cross_u, "node", axis=0, tiled=True)

    moved_table = moved_meta[:, 0]
    moved_slot = moved_meta[:, 1]
    sequence = jnp.arange(tile_count, dtype=jnp.int32)
    source = sequence // (tile_count // nodes)
    moved_rows = source * local_blocks + moved_meta[:, 2]
    picked = jnp.take(peer_rows, moved_rows, axis=0)
    products = jnp.einsum(
        "kbr,kre->kbe", moved_mult, picked, preferred_element_type=jnp.float32
    ).reshape(tile_count, -1)

    same_table = moved_table[:, None] == moved_table[None, :]
    first = jnp.min(jnp.where(same_table, sequence[None, :], tile_count), axis=1)
    first_slot = jnp.take(moved_slot, first)
    entry = moved_table * DEPTH + (moved_slot != first_slot).astype(jnp.int32)
    entries = tables * DEPTH
    chosen = entry[None, :] == jnp.arange(entries, dtype=jnp.int32)[:, None]
    send_rows = jnp.dot(
        chosen.astype(jnp.float32), products, precision=lax.Precision.HIGHEST,
        preferred_element_type=jnp.float32,
    ).astype(jnp.bfloat16)
    send_slot = jnp.max(jnp.where(chosen, moved_slot[None, :], -1), axis=1)

    arrived = lax.all_to_all(
        send_rows.reshape(tables, DEPTH, block_size, emb_width),
        "table", split_axis=0, concat_axis=0, tiled=True,
    )
    arrived_slot = lax.all_to_all(
        send_slot.reshape(tables, DEPTH), "table", split_axis=0, concat_axis=0, tiled=True
    )
    cross_out, returning = owner_work(
        arrived, arrived_slot, dense, full_v, full_u, cross_bias, cotangent
    )
    came_back = lax.all_to_all(returning, "table", split_axis=0, concat_axis=0, tiled=True)
    tile_grad = lax.dot_general(
        chosen.astype(jnp.bfloat16), came_back.reshape(entries, -1), (((0,), (0,)), ((), ())),
        preferred_element_type=jnp.float32,
    ).astype(jnp.bfloat16)
    tile_grad = lax.all_to_all(
        tile_grad.reshape(tile_count, block_size, emb_width),
        "node", split_axis=0, concat_axis=0, tiled=True,
    )
    tile_grads = jnp.einsum(
        "kbr,kbe->kre", mult_bf, tile_grad, preferred_element_type=jnp.float32
    )
    owner_rows = (
        tile_rows[None, :] == jnp.arange(local_blocks, dtype=jnp.int32)[:, None]
    ).astype(jnp.float32)
    emb_grad = jnp.dot(
        owner_rows,
        tile_grads.reshape(tile_count, -1),
        precision=lax.Precision.HIGHEST,
        preferred_element_type=jnp.float32,
    )
    return (cross_out, emb_grad.reshape(-1, emb_width))


def solution(mesh):
    in_specs = (
        P(("node", "table"), None),
        P(("node", "table"), None, None),
        P(("node", "table")),
        P(("node", "table")),
        P(("node", "table")),
        P(("node", "table"), None),
        P("node", None),
        P("node", None),
        P(),
        P(("node", "table"), None),
    )
    out_specs = (P(("node", "table"), None), P(("node", "table"), None))
    return jax.shard_map(body, mesh=mesh, in_specs=in_specs, out_specs=out_specs, check_vma=False)
```

time: 723 us -> 422 us (0.58)
  waiting for transfers between devices: 474 us -> 93.3 us
  blocking collectives: 29.5 us -> 163 us
  local copies, waits for them, and re-layouts: 82.8 us -> 50 us
  other arithmetic: 28.4 us -> 11.7 us
    all_to_all x6 -> x4, waiting for transfers between devices: 472 us -> 91.9 us  [the longest x1 91.7 us: body(): lax.all_to_all(send_rows.reshape(tables, DEPTH, block_size, emb_width), '...]
    all_to_all x1 -> x2, blocking collectives: 29.5 us -> 131 us  [the longest x1 102 us: body(): lax.all_to_all(returning, 'table', split_axis=0, concat_axis=0, tiled=True)]
    gather x8 -> x2, local copies, waits for them, and re-layouts: 37.8 us -> 2.93 us  [the longest x1 2.15 us: body(): picked = jnp.take(peer_rows, moved_rows, axis=0)]
    all_gather x0 -> x1, blocking collectives: none -> 32.1 us  [body(): peer_rows = lax.all_gather(row_blocks, 'node', axis=0, tiled=True)]
    select_n x8 -> x1, other arithmetic: 18.9 us -> 0.01 us  [body(): first_slot = jnp.take(moved_slot, first)]
    reshape x0 -> x2, local copies, waits for them, and re-layouts: none -> 9.27 us  [the longest x1 6.37 us: owner_work(): flat_arrived = arrived.reshape(-1, block_size * emb_width)]
    all_to_all x6 -> x4, local copies, waits for them, and re-layouts: 9.5 us -> 1.36 us  [the longest x2 1.27 us: body(): lax.all_to_all(send_slot.reshape(tables, DEPTH), 'table', split_axis=0, c...]
    all_to_all x6 -> x4, starting transfers between devices: 40.8 us -> 41.8 us  [the longest x1 22.1 us: body(): lax.all_to_all(send_slot.reshape(tables, DEPTH), 'table', split_axis=0, c...]
  transfers between devices with their start and end apart: 8 -> 6, of which waited for: 6 -> 2; matrix products, arithmetic and copies ran while one was open for 4% -> 12% of each run, Pallas kernels for 0% -> 0%
where the time goes in v1:
time: 422 us; the launch traced here: 421 us
  blocking collectives  163 us (39%)
  waiting for transfers between devices  93.3 us (22%)
  local copies, waits for them, and re-layouts  50 us (12%)
  matrix products  46.7 us (11%)
  starting transfers between devices  41.8 us (10%)
  between operations  14.2 us (3%)
  other arithmetic  11.7 us (3%)
    all_to_all x1, blocking collectives, body(): lax.all_to_all(returning, 'table', split_axis=0, concat_axis=0, tiled=True)  102 us
    all_to_all x1, waiting for transfers between devices, body(): lax.all_to_all(send_rows.reshape(tables, DEPTH, block_size, emb_width), '...  91.7 us
    all_gather x1, blocking collectives, body(): peer_rows = lax.all_gather(row_blocks, 'node', axis=0, tiled=True)  32.1 us
    all_to_all x1, blocking collectives, body(): lax.all_to_all(tile_grad.reshape(tile_count, block_size, emb_width), 'nod...  29 us
    all_to_all x1, starting transfers between devices, body(): lax.all_to_all(send_slot.reshape(tables, DEPTH), 'table', split_axis=0, c...  22.1 us
    unnamed x17, local copies, waits for them, and re-layouts  15.4 us
    all_to_all x1, starting transfers between devices, body(): lax.all_to_all(send_rows.reshape(tables, DEPTH, block_size, emb_width), '...  10.7 us
    dot_general x1, matrix products, owner_work(): jnp.dot(hidden, cross_u, preferred_element_type=jnp.float32) + cross_bias  8.69 us
  transfers between devices with their start and end apart: 6, of which 2 were waited for; matrix products, arithmetic and copies ran while one was open for 12% of the time, Pallas kernels for 0%

profile of v1, /device:TPU:1, one launch (start us, length us, event | category | flops | bytes accessed | tf_op | source)
XLA Modules:
  0.0 420.6 jit_solution(16068090849986939053)
XLA Ops:
  7.2 0.7 stack.12
  7.9 0.7 stack.13
  8.6 0.7 stack.14
  9.4 0.6 copy.35
  10.0 4.8 %all-to-all-start = ((s32[4,16,3]{1,2,0:T(4,128)}), s32[4,16,3]{1,2,0:T(4,128)S(1)}, u32[]{:S(2)}, u32[]{:S(2)}) async-start(s32[4,16,3]{1,2,0:T(4,128)} %copy.35), calls=%async_computation | async-start | bytes 16384 | tf_op jit(solution)/shard_map/all_to_all | solution.py:71
  14.8 4.0 convert_element_type.53
  18.8 0.0 copy-start.2
  18.8 0.2 all-to-all-done
  19.0 4.2 all-to-all-start.2
  23.2 0.0 all-gather.3.cloned.1.call-start
  23.2 0.7 all-gather.3.cloned.1.call-update
  23.9 0.0 copy-done.2
  23.9 32.1 %all_gather.9 = bf16[16,128,128]{2,1,0:T(8,128)(2,1)S(1)} all-gather(bf16[4,128,128]{2,1,0:T(8,128)(2,1)S(1)} %bitcast.101), channel_id=1, replica_groups=mesh['node'=4,'table'=64] {'node'}, dimensions={0}, use_global_device_ids=true | all-gather | bytes 655360 | tf_op jit(solution)/shard_map/all_gather | solution.py:73
  56.0 0.1 all_to_all.25
  56.1 0.2 select_reduce_fusion.1
  56.3 0.8 gather_fusion
  57.1 0.1 select_reduce_fusion
  57.2 0.8 all_to_all.26
  58.0 2.1 gather_fusion.1
  60.1 0.0 all-to-all-done.2
  60.1 22.1 %all-to-all-start.1 = ((s32[64,1,2]{2,1,0:T(1,128)}), s32[64,1,2]{2,1,0:T(1,128)S(1)}, u32[]{:S(2)}, u32[]{:S(2)}) async-start(s32[64,1,2]{2,1,0:T(1,128)} %bitcast.4), calls=%async_computation.1 | async-start | bytes 65536 | tf_op jit(solution)/shard_map/all_to_all | solution.py:103
  82.3 5.3 %convolution_bitcast_fusion.1 = f32[64,128,128]{1,2,0:T(8,128)} fusion(bf16[64,128,128]{2,1,0:T(8,128)(2,1)S(1)} %all-to-all-done.2, bf16[64,128,128]{2,1,0:T(8,128)(2,1)} %gather_fusion.1, pred[64]{0:T(512)(128)(4,1)S(1)} %get-tuple-element.2), kind=kOutput, calls=%fused_computation.25 | convolution fusion | flops 269484032 | bytes 8388672 | tf_op jit(solution)/shard_map/kbr,kre->kbe/dot_general | solution.py:83
  87.6 5.6 %copy.39 = f32[64,128,128]{2,1,0:T(8,128)} copy(f32[64,128,128]{1,2,0:T(8,128)} %convolution_bitcast_fusion.1) | data formatting | bytes 8388608 | tf_op jit(solution)/shard_map/kbr,kre->kbe/dot_general | solution.py:83
  93.2 8.5 %fusion.11 = bf16[16,8,128,128]{3,1,2,0:T(8,128)(2,1)S(1)} fusion(f32[8,8,128,128]{3,2,1,0:T(8,128)} %bitcast.91, s32[64]{0:T(128)S(1)} %multiply_add_fusion.1), kind=kOutput, calls=%fused_computation.22 | convolution fusion | flops 1612718080 | bytes 8388864 | tf_op jit(solution)/shard_map/dot_general | solution.py:93
  101.7 3.2 copy.51
  105.0 0.0 all-to-all-done.1
  105.0 10.7 %all-to-all-start.3 = ((bf16[64,2,128,128]{3,2,1,0:T(8,128)(2,1)}), bf16[64,2,128,128]{3,2,1,0:T(8,128)(2,1)}, u32[]{:S(2)}, u32[]{:S(2)}) async-start(bf16[64,2,128,128]{3,2,1,0:T(8,128)(2,1)} %bitcast.88), calls=%async_computation.3 | async-start | bytes 8388608 | tf_op jit(solution)/shard_map/all_to_all | solution.py:99
  115.6 0.0 copy-start.3
  115.6 0.0 all-gather.5.cloned.1.call-start
  115.7 0.7 all-gather.5.cloned.1.call-update
  116.4 0.0 copy-done
  116.4 2.0 convert_element_type.61
  118.4 0.0 copy-done.3
  118.5 0.5 broadcast.153
  119.0 0.7 reduce.3
  119.7 0.1 eq.77
  119.8 91.7 %all-to-all-done.3 = bf16[64,2,128,128]{3,2,1,0:T(8,128)(2,1)} async-done(((bf16[64,2,128,128]{3,2,1,0:T(8,128)(2,1)}), bf16[64,2,128,128]{3,2,1,0:T(8,128)(2,1)}, u32[]{:S(2)}, u32[]{:S(2)}) %all-to-all-start.3) | async-done | bytes 4194336 | tf_op jit(solution)/shard_map/all_to_all | solution.py:99
  211.5 7.7 %copy.77 = bf16[16,8,128,128]{3,1,2,0:T(8,128)(2,1)} copy(bf16[16,8,128,128]{3,2,1,0:T(8,128)(2,1)} %bitcast.27) | data formatting | bytes 8388608
  219.2 6.4 %copy.40 = bf16[128,16384]{0,1:T(8,128)(2,1)} copy(bf16[128,16384]{1,0:T(8,128)(2,1)} %bitcast.92) | data formatting | bytes 8388608 | tf_op jit(solution)/shard_map/reshape | solution.py:15
  225.6 3.8 convolution_convert_fusion.3
  229.4 0.8 bitcast_dynamic-update-slice_fusion
  230.2 0.0 copy-start.1
  230.2 0.0 all-gather.3.cloned.1.call-done
  230.2 1.2 copy-done.1
  231.4 6.3 %fusion.27 = f32[256,3456]{1,0:T(8,128)S(1)} fusion(bf16[3456,512]{1,0:T(8,128)(2,1)} %all-gather.3.cloned.1.call-done, bf16[512,3456]{1,0:T(8,128)(2,1)} %all-gather.5.cloned.1.call-done, bf16[256,3456]{1,0:T(8,128)(2,1)} %copy-done.1, bf16[256,3456]{1,0:T(8,128)(2,1)} %param.19), kind=kOutput, calls=%fused_computation.35 | convolution fusion | flops 1815609344 | bytes 14155776 | tf_op jit(solution)/shard_map/dot_general | solution.py:33
  237.7 8.7 %fusion.8 = (bf16[256,3456]{1,0:T(8,128)(2,1)}, f32[256,3456]{1,0:T(8,128)}) fusion(bf16[256,3456]{1,0:T(8,128)(2,1)} %copy-done.1, f32[3456]{0:T(1024)} %param.18, bf16[512,3456]{1,0:T(8,128)(2,1)} %all-gather.5.cloned.1.call-done, bf16[3456,512]{1,0:T(8,128)(2,1)} %all-gather.3.cloned.1.call-done), kind=kOutput, calls=%fused_computation.17 | convolution fusion | flops 1816494080 | bytes 14169600 | tf_op jit(solution)/shard_map/dot_general | solution.py:25
  246.4 4.6 %fusion.10 = bf16[256,3328]{1,0:T(8,128)(2,1)} fusion(f32[256,3456]{1,0:T(8,128)S(1)} %fusion.27, f32[256,3456]{1,0:T(8,128)} %get-tuple-element.7, f32[256,3456]{1,0:T(8,128)} %convert_element_type.61), kind=kLoop, calls=%fused_computation.20 | loop fusion | flops 2555904 | bytes 11927552 | tf_op jit(solution)/shard_map/convert
  251.0 2.8 copy.43
  253.8 0.4 reshape.164
  254.2 1.9 copy.44
  256.2 0.2 pad.5
  256.4 1.2 copy.54
  257.6 1.3 fusion.14
  258.9 1.2 copy.55
  260.2 101.7 %all_to_all.38 = bf16[64,2,128,128]{3,2,1,0:T(8,128)(2,1)S(1)} all-to-all(bf16[64,2,128,128]{3,2,1,0:T(8,128)(2,1)S(1)} %bitcast.93), channel_id=1, replica_groups=mesh['node'=4,'table'=64] {'table'}, dimensions={0} | all-to-all | bytes 8388608 | tf_op jit(solution)/shard_map/all_to_all | solution.py:109
  361.9 2.8 fusion.19
  364.7 0.6 copy.57
  365.3 2.9 copy.45
  368.2 29.0 %all_to_all.39 = bf16[64,128,128]{1,2,0:T(8,128)(2,1)S(1)} all-to-all(bf16[64,128,128]{1,2,0:T(8,128)(2,1)} %copy.45), channel_id=1, replica_groups=mesh['node'=4,'table'=64] {'node'}, dimensions={0} | all-to-all | bytes 4194304 | tf_op jit(solution)/shard_map/all_to_all | solution.py:114
  397.2 4.2 %convolution_bitcast_fusion = f32[64,128,128]{1,2,0:T(8,128)} fusion(bf16[64,128,128]{1,2,0:T(8,128)(2,1)S(1)} %all_to_all.39, bf16[64,128,128]{2,1,0:T(8,128)(2,1)} %convert_element_type.53), kind=kOutput, calls=%fused_computation.24 | convolution fusion | flops 268435456 | bytes 8388608 | tf_op jit(solution)/shard_map/kbr,kbe->kre/dot_general | solution.py:118
  401.5 5.6 %copy.46 = f32[64,128,128]{2,1,0:T(8,128)} copy(f32[64,128,128]{1,2,0:T(8,128)} %convolution_bitcast_fusion) | data formatting | bytes 8388608 | tf_op jit(solution)/shard_map/kbr,kbe->kre/dot_general | solution.py:118
  407.1 0.0 copy-done.4
  407.1 5.8 %fusion.1 = f32[4,16384]{1,0:T(4,128)S(1)} fusion(f32[8,8,128,128]{3,2,1,0:T(8,128)} %bitcast.94, s32[64]{0:T(128)S(1)} %copy-done.4), kind=kOutput, calls=%fused_computation.9 | convolution fusion | flops 50331904 | bytes 4456704 | tf_op jit(solution)/shard_map/dot_general | solution.py:124
  412.9 0.9 reshape.170
  (13 shorter events, 0.1 us)
Async XLA Ops:
  10.0 9.0 %all-to-all-start = ((s32[4,16,3]{1,2,0:T(4,128)}), s32[4,16,3]{1,2,0:T(4,128)S(1)}, u32[]{:S(2)}, u32[]{:S(2)}) async-start(s32[4,16,3]{1,2,0:T(4,128)} %copy.35), calls=%async_computation | async-start | bytes 16384 | tf_op jit(solution)/shard_map/all_to_all | solution.py:71
  18.8 5.1 %copy-start.2 = (bf16[512,128]{1,0:T(8,128)(2,1)S(1)}, bf16[512,128]{1,0:T(8,128)(2,1)}, u32[]{:S(2)}) copy-start(bf16[512,128]{1,0:T(8,128)(2,1)} %param.10) | copy-start | bytes 393220
  19.0 41.1 %all-to-all-start.2 = ((bf16[64,128,128]{2,1,0:T(8,128)(2,1)}), bf16[64,128,128]{2,1,0:T(8,128)(2,1)S(1)}, u32[]{:S(2)}, u32[]{:S(2)}) async-start(bf16[64,128,128]{2,1,0:T(8,128)(2,1)} %convert_element_type.53), calls=%async_computation.2 | async-start | bytes 4194304 | tf_op jit(solution)/shard_map/all_to_all | solution.py:72
  23.2 207.0 %all-gather.3.cloned.1.call-start = ((), (), s32[]{:S(2)}) async-start(), calls=%async_computation.6 | async-start | bytes 4423680 | tf_op jit(solution)/shard_map/all_gather | solution.py:74
  60.1 44.8 %all-to-all-start.1 = ((s32[64,1,2]{2,1,0:T(1,128)}), s32[64,1,2]{2,1,0:T(1,128)S(1)}, u32[]{:S(2)}, u32[]{:S(2)}) async-start(s32[64,1,2]{2,1,0:T(1,128)} %bitcast.4), calls=%async_computation.1 | async-start | bytes 65536 | tf_op jit(solution)/shard_map/all_to_all | solution.py:103
  105.0 11.4 %copy-start = (bf16[256,3456]{1,0:T(8,128)(2,1)S(1)}, bf16[256,3456]{1,0:T(8,128)(2,1)}, u32[]{:S(2)}) copy-start(bf16[256,3456]{1,0:T(8,128)(2,1)} %param.19) | copy-start | bytes 5308420
  105.0 106.5 %all-to-all-start.3 = ((bf16[64,2,128,128]{3,2,1,0:T(8,128)(2,1)}), bf16[64,2,128,128]{3,2,1,0:T(8,128)(2,1)}, u32[]{:S(2)}, u32[]{:S(2)}) async-start(bf16[64,2,128,128]{3,2,1,0:T(8,128)(2,1)} %bitcast.88), calls=%async_computation.3 | async-start | bytes 8388608 | tf_op jit(solution)/shard_map/all_to_all | solution.py:99
  115.6 2.8 copy-start.3
  115.6 115.8 %all-gather.5.cloned.1.call-start = ((), (), s32[]{:S(2)}) async-start(), calls=%async_computation.7 | async-start | bytes 4423680 | tf_op jit(solution)/shard_map/all_gather | solution.py:75
  230.2 1.2 copy-start.1
  401.5 5.6 %copy-start.4 = (s32[64]{0:T(128)S(1)}, s32[64]{0:T(128)}, u32[]{:S(2)}) copy-start(s32[64]{0:T(128)} %param.12) | copy-start | bytes 772
Sparse Core Ops, SparseCore 0:
  25.8 56.9 all-gather.2
  118.3 45.8 all-gather.4

commit v2 on v1

--- a/solution.py
+++ b/solution.py
@@ -67,17 +67,29 @@
     row_blocks = emb_rows.reshape(-1, block_size, emb_width)
     mult_bf = tile_mult.astype(jnp.bfloat16)
 
-    meta = jnp.stack([tile_table, tile_slot, tile_rows], axis=1)
-    moved_meta = lax.all_to_all(meta, "node", split_axis=0, concat_axis=0, tiled=True)
-    moved_mult = lax.all_to_all(mult_bf, "node", split_axis=0, concat_axis=0, tiled=True)
-    peer_rows = lax.all_gather(row_blocks, "node", axis=0, tiled=True)
+    per_node = tile_count // nodes
+    meta = jnp.stack([tile_table, tile_slot, tile_rows], axis=1).astype(jnp.bfloat16)
+    meta_block = jnp.zeros((nodes, block_size, emb_width), jnp.bfloat16)
+    meta_block = meta_block.at[:, :per_node, :3].set(meta.reshape(nodes, per_node, 3))
+    outgoing = jnp.concatenate(
+        [
+            mult_bf.reshape(nodes, per_node, block_size, block_size),
+            jnp.broadcast_to(row_blocks[None], (nodes, local_blocks, block_size, emb_width)),
+            meta_block[:, None],
+        ],
+        axis=1,
+    )
+    incoming = lax.all_to_all(outgoing, "node", split_axis=0, concat_axis=0, tiled=True)
     full_v = lax.all_gather(cross_v, "node", axis=0, tiled=True)
     full_u = lax.all_gather(cross_u, "node", axis=0, tiled=True)
+    moved_mult = incoming[:, :per_node].reshape(tile_count, block_size, block_size)
+    peer_rows = incoming[:, per_node:per_node + local_blocks].reshape(-1, block_size, emb_width)
+    moved_meta = incoming[:, -1, :per_node, :3].reshape(tile_count, 3).astype(jnp.int32)
 
     moved_table = moved_meta[:, 0]
     moved_slot = moved_meta[:, 1]
     sequence = jnp.arange(tile_count, dtype=jnp.int32)
-    source = sequence // (tile_count // nodes)
+    source = sequence // per_node
     moved_rows = source * local_blocks + moved_meta[:, 2]
     picked = jnp.take(peer_rows, moved_rows, axis=0)
     products = jnp.einsum(

time: 422 us -> 434 us (1.028)
  waiting for transfers between devices: 93.3 us -> 128 us
  blocking collectives: 163 us -> 131 us
  local copies, waits for them, and re-layouts: 50 us -> 63.7 us
  matrix products: 46.7 us -> 41.6 us
  other arithmetic: 11.7 us -> 16.7 us
  starting transfers between devices: 41.8 us -> 37.2 us
    all_to_all x2 -> x1, waiting for transfers between devices: 0.18 us -> 37.6 us  [body(): lax.all_to_all(outgoing, 'node', split_axis=0, concat_axis=0, tiled=True)]
    all_gather x1 -> x0, blocking collectives: 32.1 us -> none  [body(): peer_rows = lax.all_gather(row_blocks, 'node', axis=0, tiled=True)]
    dot_general x1 -> x0, local copies, waits for them, and re-layouts: 5.63 us -> none  [body(): jnp.einsum('kbr,kre->kbe', moved_mult, picked, preferred_element_type=jnp...]
    concatenate x0 -> x1, local copies, waits for them, and re-layouts: none -> 4.5 us  [body(): jnp.concatenate([mult_bf.reshape(nodes, per_node, block_size, block_size)...]
    dot_general x1, matrix products: 5.32 us -> 0.94 us  [body(): jnp.einsum('kbr,kre->kbe', moved_mult, picked, preferred_element_type=jnp...]
    all_to_all x2 -> x1, starting transfers between devices: 9.04 us -> 4.84 us  [body(): lax.all_to_all(outgoing, 'node', split_axis=0, concat_axis=0, tiled=True)]
    unnamed x17 -> x18, local copies, waits for them, and re-layouts: 15.4 us -> 18.2 us
  transfers between devices with their start and end apart: 6 -> 5, of which waited for: 2 -> 2; matrix products, arithmetic and copies ran while one was open for 12% -> 10% of each run, Pallas kernels for 0% -> 0%
where the time goes in v2:
time: 434 us; the launch traced here: 433 us
  blocking collectives  131 us (30%)
  waiting for transfers between devices  128 us (29%)
  local copies, waits for them, and re-layouts  63.7 us (15%)
  matrix products  41.6 us (10%)
  starting transfers between devices  37.2 us (9%)
  other arithmetic  16.7 us (4%)
  between operations  14.2 us (3%)
    all_to_all x1, blocking collectives, body(): lax.all_to_all(returning, 'table', split_axis=0, concat_axis=0, tiled=True)  102 us
    all_to_all x1, waiting for transfers between devices, body(): lax.all_to_all(send_rows.reshape(tables, DEPTH, block_size, emb_width), '...  89.6 us
    all_to_all x1, waiting for transfers between devices, body(): lax.all_to_all(outgoing, 'node', split_axis=0, concat_axis=0, tiled=True)  37.6 us
    all_to_all x1, blocking collectives, body(): lax.all_to_all(tile_grad.reshape(tile_count, block_size, emb_width), 'nod...  29.6 us
    all_to_all x1, starting transfers between devices, body(): lax.all_to_all(send_slot.reshape(tables, DEPTH), 'table', split_axis=0, c...  21.6 us
    unnamed x18, local copies, waits for them, and re-layouts  18.2 us
    all_to_all x1, starting transfers between devices, body(): lax.all_to_all(send_rows.reshape(tables, DEPTH, block_size, emb_width), '...  10.5 us
  transfers between devices with their start and end apart: 5, of which 2 were waited for; matrix products, arithmetic and copies ran while one was open for 10% of the time, Pallas kernels for 0%

profile of v2, /device:TPU:1, one launch (start us, length us, event | category | flops | bytes accessed | tf_op | source)
XLA Modules:
  0.0 433.1 jit_solution(1836985401723522767)
XLA Ops:
  7.2 0.0 copy-start.1
  7.2 0.7 convert.16
  7.9 0.1 stack.12
  8.0 0.7 convert.17
  8.6 0.1 stack.13
  8.7 0.7 convert.18
  9.4 0.1 stack.14
  9.5 0.1 copy.81
  9.6 2.7 convert_element_type.67
  12.3 0.1 broadcast_in_dim.57
  12.4 1.7 fusion.12
  14.1 4.5 %copy.82 = bf16[4,21,128,128]{2,3,1,0:T(8,128)(2,1)} copy(bf16[4,21,128,128]{3,2,1,0:T(8,128)(2,1)} %fusion.12) | data formatting | bytes 5505024 | tf_op jit(solution)/shard_map/concatenate | solution.py:74
  18.6 4.8 %all-to-all-start = ((bf16[4,21,128,128]{2,3,1,0:T(8,128)(2,1)}), bf16[4,21,128,128]{2,3,1,0:T(8,128)(2,1)}, u32[]{:S(2)}, u32[]{:S(2)}) async-start(bf16[4,21,128,128]{2,3,1,0:T(8,128)(2,1)} %copy.82), calls=%async_computation | async-start | bytes 5505024 | tf_op jit(solution)/shard_map/all_to_all | solution.py:82
  23.4 0.7 all-gather.3.cloned.1.call-update
  24.2 37.6 %all-to-all-done = bf16[4,21,128,128]{2,3,1,0:T(8,128)(2,1)} async-done(((bf16[4,21,128,128]{2,3,1,0:T(8,128)(2,1)}), bf16[4,21,128,128]{2,3,1,0:T(8,128)(2,1)}, u32[]{:S(2)}, u32[]{:S(2)}) %all-to-all-start) | async-done | bytes 2752544 | tf_op jit(solution)/shard_map/all_to_all | solution.py:82
  61.8 0.7 slice.58
  62.5 0.1 reshape.267
  62.6 0.2 select_reduce_fusion.1
  62.8 0.8 gather_fusion
  63.6 0.1 select_reduce_fusion
  63.7 0.8 all_to_all.19
  64.5 21.6 %all-to-all-start.1 = ((s32[64,1,2]{2,1,0:T(1,128)}), s32[64,1,2]{2,1,0:T(1,128)S(1)}, u32[]{:S(2)}, u32[]{:S(2)}) async-start(s32[64,1,2]{2,1,0:T(1,128)} %bitcast.6), calls=%async_computation.1 | async-start | bytes 65536 | tf_op jit(solution)/shard_map/all_to_all | solution.py:115
  86.1 1.1 slice.60
  87.1 0.3 copy.98
  87.4 2.2 gather_fusion.1
  89.6 1.9 slice.59
  91.5 0.3 copy-done
  91.8 0.9 fusion.17
  92.8 7.6 %fusion.13 = bf16[16,8,128,128]{3,1,2,0:T(8,128)(2,1)S(1)} fusion(f32[8,8,128,128]{3,2,1,0:T(8,128)S(1)} %bitcast.92, s32[64]{0:T(128)S(1)} %multiply_add_fusion.1), kind=kOutput, calls=%fused_computation.25 | convolution fusion | flops 1612718080 | bytes 8388864 | tf_op jit(solution)/shard_map/dot_general | solution.py:105
  100.3 3.2 copy.100
  103.6 0.0 all-to-all-done.1
  103.6 10.5 %all-to-all-start.2 = ((bf16[64,2,128,128]{3,2,1,0:T(8,128)(2,1)}), bf16[64,2,128,128]{3,2,1,0:T(8,128)(2,1)}, u32[]{:S(2)}, u32[]{:S(2)}) async-start(bf16[64,2,128,128]{3,2,1,0:T(8,128)(2,1)} %bitcast.91), calls=%async_computation.2 | async-start | bytes 8388608 | tf_op jit(solution)/shard_map/all_to_all | solution.py:111
  114.1 0.0 copy-start.2
  114.1 0.2 all-gather.5.cloned.1.call-start
  114.3 0.5 all-gather.5.cloned.1.call-update
  114.8 3.5 convert_element_type.78
  118.4 0.7 constant_dynamic-update-slice_fusion
  119.0 0.5 broadcast.191
  119.5 0.7 reduce.5
  120.3 0.1 eq.77
  120.4 89.6 %all-to-all-done.2 = bf16[64,2,128,128]{3,2,1,0:T(8,128)(2,1)} async-done(((bf16[64,2,128,128]{3,2,1,0:T(8,128)(2,1)}), bf16[64,2,128,128]{3,2,1,0:T(8,128)(2,1)}, u32[]{:S(2)}, u32[]{:S(2)}) %all-to-all-start.2) | async-done | bytes 4194336 | tf_op jit(solution)/shard_map/all_to_all | solution.py:111
  210.0 7.7 %copy.127 = bf16[16,8,128,128]{3,1,2,0:T(8,128)(2,1)} copy(bf16[16,8,128,128]{3,2,1,0:T(8,128)(2,1)} %bitcast.30) | data formatting | bytes 8388608
  217.7 6.4 %copy.87 = bf16[128,16384]{0,1:T(8,128)(2,1)} copy(bf16[128,16384]{1,0:T(8,128)(2,1)} %bitcast.95) | data formatting | bytes 8388608 | tf_op jit(solution)/shard_map/reshape | solution.py:15
  224.0 3.8 convolution_convert_fusion.3
  227.8 1.9 bitcast_dynamic-update-slice_fusion
  229.8 8.1 %fusion.30 = f32[256,3456]{1,0:T(8,128)} fusion(bf16[3456,512]{1,0:T(8,128)(2,1)} %all-gather.3.cloned.1.call-done, bf16[512,3456]{1,0:T(8,128)(2,1)} %all-gather.5.cloned.1.call-done, bf16[256,3456]{1,0:T(8,128)(2,1)} %bitcast_dynamic-update-slice_fusion, bf16[256,3456]{1,0:T(8,128)(2,1)} %param.21), kind=kOutput, calls=%fused_computation.38 | convolution fusion | flops 1815609344 | bytes 14155776 | tf_op jit(solution)/shard_map/dot_general | solution.py:33
  237.9 8.7 %fusion.9 = (bf16[256,3456]{1,0:T(8,128)(2,1)}, f32[256,3456]{1,0:T(8,128)}) fusion(bf16[256,3456]{1,0:T(8,128)(2,1)} %bitcast_dynamic-update-slice_fusion, f32[3456]{0:T(1024)S(1)} %copy-done.4, bf16[512,3456]{1,0:T(8,128)(2,1)} %all-gather.5.cloned.1.call-done, bf16[3456,512]{1,0:T(8,128)(2,1)} %all-gather.3.cloned.1.call-done), kind=kOutput, calls=%fused_computation.19 | convolution fusion | flops 1816494080 | bytes 14169600 | tf_op jit(solution)/shard_map/dot_general | solution.py:25
  246.5 5.7 %fusion.11 = bf16[256,3328]{1,0:T(8,128)(2,1)} fusion(f32[256,3456]{1,0:T(8,128)} %fusion.30, f32[256,3456]{1,0:T(8,128)} %get-tuple-element.19, f32[256,3456]{1,0:T(8,128)} %convert_element_type.78), kind=kLoop, calls=%fused_computation.22 | loop fusion | flops 2555904 | bytes 11927552 | tf_op jit(solution)/shard_map/convert.1
  252.2 3.8 copy.90
  256.0 4.4 %reshape.260 = bf16[2,128,26,128]{1,0,3,2:T(2,128)(2,1)} reshape(bf16[256,3328]{0,1:T(8,128)(2,1)} %copy.90) | data formatting | bytes 3407872 | tf_op jit(solution)/shard_map/reshape | solution.py:39
  260.4 5.3 %copy.91 = bf16[26,2,128,128]{3,2,1,0:T(8,128)(2,1)} copy(bf16[26,2,128,128]{2,1,3,0:T(2,128)(2,1)} %bitcast.105) | data formatting | bytes 3407872 | tf_op jit(solution)/shard_map/transpose | solution.py:41
  265.7 1.7 pad.14
  267.4 1.2 copy.103
  268.6 1.3 fusion.16
  269.9 1.2 copy.104
  271.2 101.7 %all_to_all.29 = bf16[64,2,128,128]{3,2,1,0:T(8,128)(2,1)S(1)} all-to-all(bf16[64,2,128,128]{3,2,1,0:T(8,128)(2,1)S(1)} %bitcast.96), channel_id=1, replica_groups=mesh['node'=4,'table'=64] {'table'}, dimensions={0} | all-to-all | bytes 8388608 | tf_op jit(solution)/shard_map/all_to_all | solution.py:121
  372.9 2.8 fusion.22
  375.7 1.9 copy.106
  377.6 4.1 copy.92
  381.7 29.6 %all_to_all.30 = bf16[64,128,128]{1,2,0:T(8,128)(2,1)S(1)} all-to-all(bf16[64,128,128]{1,2,0:T(8,128)(2,1)} %copy.92), channel_id=1, replica_groups=mesh['node'=4,'table'=64] {'node'}, dimensions={0} | all-to-all | bytes 4194304 | tf_op jit(solution)/shard_map/all_to_all | solution.py:126
  411.3 2.7 convolution_bitcast_fusion
  414.0 5.6 %copy.93 = f32[64,128,128]{2,1,0:T(8,128)} copy(f32[64,128,128]{1,2,0:T(8,128)} %convolution_bitcast_fusion) | data formatting | bytes 8388608 | tf_op jit(solution)/shard_map/kbr,kbe->kre/dot_general | solution.py:130
  419.6 5.8 %fusion.2 = f32[4,16384]{1,0:T(4,128)S(1)} fusion(f32[8,8,128,128]{3,2,1,0:T(8,128)} %bitcast.97, s32[64]{0:T(128)S(1)} %copy-done.3), kind=kOutput, calls=%fused_computation.11 | convolution fusion | flops 50331904 | bytes 4456704 | tf_op jit(solution)/shard_map/dot_general | solution.py:136
  425.4 0.9 reshape.266
  (18 shorter events, 0.1 us)
Async XLA Ops:
  7.2 5.1 %copy-start.1 = (bf16[512,128]{1,0:T(8,128)(2,1)S(1)}, bf16[512,128]{1,0:T(8,128)(2,1)}, u32[]{:S(2)}) copy-start(bf16[512,128]{1,0:T(8,128)(2,1)} %param.12) | copy-start | bytes 393220
  18.6 43.2 %all-to-all-start = ((bf16[4,21,128,128]{2,3,1,0:T(8,128)(2,1)}), bf16[4,21,128,128]{2,3,1,0:T(8,128)(2,1)}, u32[]{:S(2)}, u32[]{:S(2)}) async-start(bf16[4,21,128,128]{2,3,1,0:T(8,128)(2,1)} %copy.82), calls=%async_computation | async-start | bytes 5505024 | tf_op jit(solution)/shard_map/all_to_all | solution.py:82
  23.4 206.4 %all-gather.3.cloned.1.call-start = ((), (), s32[]{:S(2)}) async-start(), calls=%async_computation.5 | async-start | bytes 4423680 | tf_op jit(solution)/shard_map/all_gather | solution.py:83
  64.5 39.1 %all-to-all-start.1 = ((s32[64,1,2]{2,1,0:T(1,128)}), s32[64,1,2]{2,1,0:T(1,128)S(1)}, u32[]{:S(2)}, u32[]{:S(2)}) async-start(s32[64,1,2]{2,1,0:T(1,128)} %bitcast.6), calls=%async_computation.1 | async-start | bytes 65536 | tf_op jit(solution)/shard_map/all_to_all | solution.py:115
  89.6 2.2 copy-start
  103.6 106.4 %all-to-all-start.2 = ((bf16[64,2,128,128]{3,2,1,0:T(8,128)(2,1)}), bf16[64,2,128,128]{3,2,1,0:T(8,128)(2,1)}, u32[]{:S(2)}, u32[]{:S(2)}) async-start(bf16[64,2,128,128]{3,2,1,0:T(8,128)(2,1)} %bitcast.91), calls=%async_computation.2 | async-start | bytes 8388608 | tf_op jit(solution)/shard_map/all_to_all | solution.py:111
  114.1 4.3 copy-start.2
  114.1 115.7 %all-gather.5.cloned.1.call-start = ((), (), s32[]{:S(2)}) async-start(), calls=%async_computation.6 | async-start | bytes 4423680 | tf_op jit(solution)/shard_map/all_gather | solution.py:84
  229.8 8.1 %copy-start.4 = (f32[3456]{0:T(1024)S(1)}, f32[3456]{0:T(1024)}, u32[]{:S(2)}) copy-start(f32[3456]{0:T(1024)} %param.20) | copy-start | bytes 41476
  414.0 5.7 %copy-start.3 = (s32[64]{0:T(128)S(1)}, s32[64]{0:T(128)}, u32[]{:S(2)}) copy-start(s32[64]{0:T(128)} %param.14) | copy-start | bytes 772
Sparse Core Ops, SparseCore 0:
  26.1 60.3 all-gather.2
  116.7 43.9 all-gather.4

commit v3 on v2

--- a/solution.py
+++ b/solution.py
@@ -1,6 +1,8 @@
 import jax
 import jax.numpy as jnp
 from jax import lax
+from jax.experimental import pallas as pl
+from jax.experimental.pallas import tpu as pltpu
 from jax.sharding import PartitionSpec as P
 
 FEATURES = 26
@@ -9,40 +11,109 @@
 BAG_BLOCKS = 52
 
 
+def cross_kernel(
+    slot_ref, arrived_ref, dense_ref, v_ref, u_ref, bias_ref, cot_ref,
+    out_ref, ret_ref, pooled_ref, layer_ref, dscale_ref, dlayer_ref, bag_ref,
+):
+    entries, block_size, emb_width = arrived_ref.shape
+    bags = pooled_ref.shape[0]
+    chunks = layer_ref.shape[1] // emb_width
+    f32, bf16 = jnp.float32, jnp.bfloat16
+
+    pooled_ref[...] = jnp.zeros_like(pooled_ref)
+
+    def pool(i, carry):
+        slot = slot_ref[i]
+
+        @pl.when(slot >= 0)
+        def _():
+            pooled_ref[slot] += arrived_ref[i].astype(f32)
+
+        return carry
+
+    lax.fori_loop(0, entries, pool, 0)
+    layer_ref[:, 0:emb_width] = dense_ref[...]
+    for bag in range(bags):
+        feature, half = divmod(bag, SAMPLE_BLOCKS)
+        layer_ref[
+            half * block_size:(half + 1) * block_size,
+            (feature + 1) * emb_width:(feature + 2) * emb_width,
+        ] = pooled_ref[bag].astype(bf16)
+
+    hidden = jnp.dot(layer_ref[...], v_ref[...], preferred_element_type=f32).astype(bf16)
+
+    def forward(c, carry):
+        cols = pl.ds(pl.multiple_of(c * emb_width, emb_width), emb_width)
+        scale = jnp.dot(hidden, u_ref[:, cols], preferred_element_type=f32) + bias_ref[:, cols]
+        layer_input = layer_ref[:, cols].astype(f32)
+        upstream = cot_ref[:, cols].astype(f32)
+        out_ref[:, cols] = (layer_input * (scale + 1.0)).astype(bf16)
+        dscale_ref[:, cols] = (upstream * layer_input).astype(bf16)
+        dlayer_ref[:, cols] = upstream * (scale + 1.0)
+        return carry
+
+    lax.fori_loop(0, chunks, forward, 0)
+    dhidden = lax.dot_general(
+        dscale_ref[...], u_ref[...], (((1,), (1,)), ((), ())), preferred_element_type=f32
+    ).astype(bf16)
+
+    def backward(feature, carry):
+        start = pl.multiple_of((feature + 1) * emb_width, emb_width)
+        cols = pl.ds(start, emb_width)
+        dlayer = dlayer_ref[:, cols] + lax.dot_general(
+            dhidden, v_ref[cols, :], (((1,), (1,)), ((), ())), preferred_element_type=f32
+        )
+        grad = dlayer.astype(bf16)
+        for half in range(SAMPLE_BLOCKS):
+            bag_ref[feature * SAMPLE_BLOCKS + half] = grad[half * block_size:(half + 1) * block_size]
+        return carry
+
+    lax.fori_loop(0, chunks - 1, backward, 0)
+
+    def gather_back(i, carry):
+        slot = slot_ref[i]
+        picked = bag_ref[jnp.maximum(slot, 0)]
+        ret_ref[i] = jnp.where(slot >= 0, picked, jnp.zeros_like(picked))
+        return carry
+
+    lax.fori_loop(0, entries, gather_back, 0)
+
+
 def owner_work(arrived, arrived_slot, dense, cross_v, cross_u, cross_bias, cotangent):
     block_size = arrived.shape[-2]
     emb_width = arrived.shape[-1]
-    flat_arrived = arrived.reshape(-1, block_size * emb_width)
-    flat_slot = arrived_slot.reshape(-1)
-    selector = flat_slot[None, :] == jnp.arange(BAG_BLOCKS, dtype=jnp.int32)[:, None]
-    pooled = jnp.dot(
-        selector.astype(jnp.bfloat16), flat_arrived, preferred_element_type=jnp.float32
-    )
-    embedded = pooled.reshape(FEATURES, SAMPLE_BLOCKS, block_size, emb_width).transpose(1, 2, 0, 3)
-    embedded = embedded.reshape(-1, FEATURES * emb_width).astype(jnp.bfloat16)
-    first_layer = jnp.concatenate([dense, embedded], axis=1)
-    hidden = jnp.dot(first_layer, cross_v, preferred_element_type=jnp.float32).astype(jnp.bfloat16)
-    cross_scale = jnp.dot(hidden, cross_u, preferred_element_type=jnp.float32) + cross_bias
-    layer_input = first_layer.astype(jnp.float32)
-    cross_out = (layer_input * (cross_scale + 1.0)).astype(jnp.bfloat16)
-    upstream = cotangent.astype(jnp.float32)
-    dscale = (upstream * layer_input).astype(jnp.bfloat16)
-    dhidden = lax.dot_general(
-        dscale, cross_u, (((1,), (1,)), ((), ())), preferred_element_type=jnp.float32
-    ).astype(jnp.bfloat16)
-    dlayer = upstream * (cross_scale + 1.0) + lax.dot_general(
-        dhidden, cross_v, (((1,), (1,)), ((), ())), preferred_element_type=jnp.float32
-    )
-    bag_grad = (
-        dlayer[:, emb_width:]
-        .astype(jnp.bfloat16)
-        .reshape(SAMPLE_BLOCKS, block_size, FEATURES, emb_width)
-    )
-    bag_grad = bag_grad.transpose(2, 0, 1, 3).reshape(BAG_BLOCKS, block_size * emb_width)
-    returning = lax.dot_general(
-        selector.astype(jnp.bfloat16), bag_grad, (((0,), (0,)), ((), ())),
-        preferred_element_type=jnp.float32,
-    ).astype(jnp.bfloat16)
+    entries = arrived.shape[0] * arrived.shape[1]
+    samples, width = cotangent.shape
+    rank = cross_v.shape[1]
+    vmem = pl.BlockSpec(memory_space=pltpu.VMEM)
+    flops = 8 * samples * width * rank
+    nbytes = 2 * (2 * entries * block_size * emb_width + 2 * width * rank + 2 * samples * width)
+    cross_out, returning = pl.pallas_call(
+        cross_kernel,
+        out_shape=(
+            jax.ShapeDtypeStruct((samples, width), jnp.bfloat16),
+            jax.ShapeDtypeStruct((entries, block_size, emb_width), jnp.bfloat16),
+        ),
+        in_specs=[pl.BlockSpec(memory_space=pltpu.SMEM)] + [vmem] * 6,
+        out_specs=(vmem, vmem),
+        scratch_shapes=[
+            pltpu.VMEM((BAG_BLOCKS, block_size, emb_width), jnp.float32),
+            pltpu.VMEM((samples, width), jnp.bfloat16),
+            pltpu.VMEM((samples, width), jnp.bfloat16),
+            pltpu.VMEM((samples, width), jnp.float32),
+            pltpu.VMEM((BAG_BLOCKS, block_size, emb_width), jnp.bfloat16),
+        ],
+        compiler_params=pltpu.CompilerParams(vmem_limit_bytes=64 * 1024 * 1024),
+        cost_estimate=pl.CostEstimate(flops=flops, bytes_accessed=nbytes, transcendentals=0),
+    )(
+        arrived_slot.reshape(-1),
+        arrived.reshape(entries, block_size, emb_width),
+        dense,
+        cross_v,
+        cross_u,
+        cross_bias.reshape(1, -1),
+        cotangent,
+    )
     return cross_out, returning.reshape(arrived.shape)
 
 

time: 434 us -> 394 us (0.908)
  local copies, waits for them, and re-layouts: 63.7 us -> 26.9 us
  Pallas kernels: 0 us -> 26.2 us
  matrix products: 41.6 us -> 19.7 us
  other arithmetic: 16.7 us -> 6.11 us
    all_gather x1, waiting for transfers between devices: 0.01 us -> 43.4 us  [body(): full_u = lax.all_gather(cross_u, 'node', axis=0, tiled=True)]
    all_to_all x1, waiting for transfers between devices: 89.6 us -> 49.3 us  [body(): lax.all_to_all(send_rows.reshape(tables, DEPTH, block_size, emb_width), '...]
    pallas_call x0 -> x1, Pallas kernels: none -> 26.2 us  [owner_work(): pl.pallas_call(cross_kernel, out_shape=(jax.ShapeDtypeStruct((samples, wi...]
    dot_general x4 -> x0, matrix products: 21.8 us -> none  [the longest x1 8.66 us: owner_work(): jnp.dot(hidden, cross_u, preferred_element_type=jnp.float32) + cross_bias]
    unnamed x18 -> x19, local copies, waits for them, and re-layouts: 18.2 us -> 7.66 us
    reshape x2, local copies, waits for them, and re-layouts: 10.7 us -> 1.26 us  [the longest x1 0.65 us: owner_work(): arrived_slot.reshape(-1)]
    another operation x4 -> x3, other arithmetic: 7.73 us -> 1.98 us
    transpose x1 -> x0, local copies, waits for them, and re-layouts: 5.34 us -> none  [owner_work(): bag_grad.transpose(2, 0, 1, 3).reshape(BAG_BLOCKS, block_size * emb_width)]
  transfers between devices with their start and end apart: 5 -> 5, of which waited for: 2 -> 3; matrix products, arithmetic and copies ran while one was open for 10% -> 5% of each run, Pallas kernels for 0% -> 0%
where the time goes in v3:
time: 394 us; the launch traced here: 393 us
  waiting for transfers between devices  132 us (34%)
  blocking collectives  132 us (34%)
  starting transfers between devices  36 us (9%)
  local copies, waits for them, and re-layouts  26.9 us (7%)
  Pallas kernels  26.2 us (7%)
  matrix products  19.7 us (5%)
  between operations  14.2 us (4%)
  other arithmetic  6.11 us (2%)
    all_to_all x1, blocking collectives, body(): lax.all_to_all(returning, 'table', split_axis=0, concat_axis=0, tiled=True)  102 us
    all_to_all x1, waiting for transfers between devices, body(): lax.all_to_all(send_rows.reshape(tables, DEPTH, block_size, emb_width), '...  49.3 us
    all_gather x1, waiting for transfers between devices, body(): full_u = lax.all_gather(cross_u, 'node', axis=0, tiled=True)  43.4 us
    all_to_all x1, waiting for transfers between devices, body(): lax.all_to_all(outgoing, 'node', split_axis=0, concat_axis=0, tiled=True)  38.4 us
    all_to_all x1, blocking collectives, body(): lax.all_to_all(tile_grad.reshape(tile_count, block_size, emb_width), 'nod...  29.8 us
    pallas_call x1, Pallas kernels, owner_work(): pl.pallas_call(cross_kernel, out_shape=(jax.ShapeDtypeStruct((samples, wi...  26.2 us
    all_to_all x1, starting transfers between devices, body(): lax.all_to_all(send_slot.reshape(tables, DEPTH), 'table', split_axis=0, c...  20.3 us
    all_to_all x1, starting transfers between devices, body(): lax.all_to_all(send_rows.reshape(tables, DEPTH, block_size, emb_width), '...  10.6 us
  transfers between devices with their start and end apart: 5, of which 3 were waited for; matrix products, arithmetic and copies ran while one was open for 5% of the time, Pallas kernels for 0%

profile of v3, /device:TPU:1, one launch (start us, length us, event | category | flops | bytes accessed | tf_op | source)
XLA Modules:
  0.0 393.2 jit_solution(11287738884541201510)
XLA Ops:
  7.2 0.7 convert.13
  7.8 0.1 stack.12
  7.9 0.7 convert.14
  8.6 0.1 stack.13
  8.7 0.7 convert.15
  9.3 0.1 stack.14
  9.4 0.1 copy.50
  9.5 0.0 copy-start.3
  9.5 2.7 convert_element_type.34
  12.3 0.0 copy-start
  12.3 0.0 copy-done.3
  12.3 0.1 broadcast_in_dim.55
  12.4 1.2 copy-done
  13.6 0.4 fusion.8
  13.9 2.7 copy.51
  16.6 4.8 %all-to-all-start = ((bf16[4,21,128,128]{2,3,1,0:T(8,128)(2,1)}), bf16[4,21,128,128]{2,3,1,0:T(8,128)(2,1)S(1)}, u32[]{:S(2)}, u32[]{:S(2)}) async-start(bf16[4,21,128,128]{2,3,1,0:T(8,128)(2,1)} %copy.51), calls=%async_computation | async-start | bytes 5505024 | tf_op jit(solution)/shard_map/all_to_all | solution.py:153
  21.5 0.0 all-gather.3.cloned.1.call-start
  21.5 0.7 all-gather.3.cloned.1.call-update
  22.2 38.4 %all-to-all-done = bf16[4,21,128,128]{2,3,1,0:T(8,128)(2,1)S(1)} async-done(((bf16[4,21,128,128]{2,3,1,0:T(8,128)(2,1)}), bf16[4,21,128,128]{2,3,1,0:T(8,128)(2,1)S(1)}, u32[]{:S(2)}, u32[]{:S(2)}) %all-to-all-start) | async-done | bytes 2752544 | tf_op jit(solution)/shard_map/all_to_all | solution.py:153
  60.6 0.1 reshape.243
  60.7 0.2 select_reduce_fusion.1
  60.9 0.8 gather_fusion
  61.7 0.0 copy-start.5
  61.7 0.1 select_reduce_fusion
  61.8 0.8 all_to_all.19
  62.5 20.3 %all-to-all-start.1 = ((s32[64,1,2]{2,1,0:T(1,128)}), s32[64,1,2]{2,1,0:T(1,128)S(1)}, u32[]{:S(2)}, u32[]{:S(2)}) async-start(s32[64,1,2]{2,1,0:T(1,128)} %bitcast.6), calls=%async_computation.1 | async-start | bytes 65536 | tf_op jit(solution)/shard_map/all_to_all | solution.py:186
  82.8 0.8 slice.55
  83.6 1.3 copy.60
  85.0 2.2 gather_fusion.1
  87.2 0.0 copy-start.2
  87.2 0.2 slice.54
  87.4 1.3 copy-done.2
  88.8 0.9 fusion.12
  89.7 0.0 copy-done.5
  89.7 7.6 %fusion.9 = bf16[16,8,128,128]{3,1,2,0:T(8,128)(2,1)S(1)} fusion(f32[8,8,128,128]{3,2,1,0:T(8,128)S(1)} %bitcast.56, s32[64]{0:T(128)S(1)} %multiply_add_fusion), kind=kOutput, calls=%fused_computation.14 | convolution fusion | flops 1612718080 | bytes 8388864 | tf_op jit(solution)/shard_map/dot_general | solution.py:176
  97.3 3.2 copy.62
  100.5 0.0 all-to-all-done.1
  100.5 0.0 copy-start.4
  100.6 10.6 %all-to-all-start.2 = ((bf16[64,2,128,128]{3,2,1,0:T(8,128)(2,1)}), bf16[64,2,128,128]{3,2,1,0:T(8,128)(2,1)}, u32[]{:S(2)}, u32[]{:S(2)}) async-start(bf16[64,2,128,128]{3,2,1,0:T(8,128)(2,1)} %bitcast.55), calls=%async_computation.2 | async-start | bytes 8388608 | tf_op jit(solution)/shard_map/all_to_all | solution.py:182
  111.2 0.2 all-gather.5.cloned.1.call-start
  111.4 0.5 all-gather.5.cloned.1.call-update
  112.0 0.0 copy-done.4
  112.0 0.6 reshape.237.bias_ref
  112.6 0.5 broadcast.167
  113.1 0.7 reduce.5
  113.8 0.7 reshape.231.slot_ref
  114.5 0.0 all-gather.3.cloned.1.call-done.v_ref
  114.5 43.4 %all-gather.5.cloned.1.call-done.u_ref = bf16[512,3456]{1,0:T(8,128)(2,1)} async-done(((bf16[128,3456]{1,0:T(8,128)(2,1)}), bf16[512,3456]{1,0:T(8,128)(2,1)}) %all-gather.5.cloned.1.call-update) | async-done | bytes 3538960 | tf_op jit(solution)/shard_map/all_gather | solution.py:155
  157.8 49.3 %all-to-all-done.2 = bf16[64,2,128,128]{3,2,1,0:T(8,128)(2,1)} async-done(((bf16[64,2,128,128]{3,2,1,0:T(8,128)(2,1)}), bf16[64,2,128,128]{3,2,1,0:T(8,128)(2,1)}, u32[]{:S(2)}, u32[]{:S(2)}) %all-to-all-start.2) | async-done | bytes 4194336 | tf_op jit(solution)/shard_map/all_to_all | solution.py:182
  207.1 26.2 %shard_map.113 = (bf16[256,3456]{1,0:T(8,128)(2,1)}, bf16[128,128,128]{2,1,0:T(8,128)(2,1)}) custom-call(s32[128]{0:T(128)} %reshape.231.slot_ref, bf16[128,128,128]{2,1,0:T(8,128)(2,1)} %bitcast.11.arrived_ref, bf16[256,128]{1,0:T(8,128)(2,1)} %dense_ref.1, bf16[3456,512]{1,0:T(8,128)(2,1)} %all-gather.3.cloned.1.call-done.v_ref, ...), custom_call_target="tpu_custom_call" | custom-call | flops 3623878656 | bytes 19005440 | tf_op jit(solution)/shard_map/pallas_call | solution.py:91
  233.3 0.0 copy-start.6
  233.3 102.1 %all_to_all.29 = bf16[64,2,128,128]{3,2,1,0:T(8,128)(2,1)S(1)} all-to-all(bf16[64,2,128,128]{3,2,1,0:T(8,128)(2,1)} %bitcast.62), channel_id=1, replica_groups=mesh['node'=4,'table'=64] {'table'}, dimensions={0} | all-to-all | bytes 8388608 | tf_op jit(solution)/shard_map/all_to_all | solution.py:192
  335.4 0.0 copy-done.6
  335.4 2.8 fusion.15
  338.2 0.6 copy.64
  338.8 2.9 copy.56
  341.7 0.0 copy-start.1
  341.7 29.8 %all_to_all.30 = bf16[64,128,128]{1,2,0:T(8,128)(2,1)S(1)} all-to-all(bf16[64,128,128]{1,2,0:T(8,128)(2,1)} %copy.56), channel_id=1, replica_groups=mesh['node'=4,'table'=64] {'node'}, dimensions={0} | all-to-all | bytes 4194304 | tf_op jit(solution)/shard_map/all_to_all | solution.py:197
  371.4 0.0 copy-done.1
  371.4 2.6 convolution_bitcast_fusion
  374.1 5.7 %copy.57 = f32[64,128,128]{2,1,0:T(8,128)} copy(f32[64,128,128]{1,2,0:T(8,128)} %convolution_bitcast_fusion) | data formatting | bytes 8388608 | tf_op jit(solution)/shard_map/kbr,kbe->kre/dot_general | solution.py:201
  379.7 0.0 copy-done.7
  379.7 5.8 %fusion.1 = f32[4,16384]{1,0:T(4,128)S(1)} fusion(f32[8,8,128,128]{3,2,1,0:T(8,128)} %bitcast.58, s32[64]{0:T(128)S(1)} %copy-done.7), kind=kOutput, calls=%fused_computation.6 | convolution fusion | flops 50331904 | bytes 4456704 | tf_op jit(solution)/shard_map/dot_general | solution.py:207
  385.5 0.9 reshape.242
  (10 shorter events, 0.1 us)
Async XLA Ops:
  9.5 2.7 copy-start.3
  12.3 1.3 copy-start
  16.6 43.9 %all-to-all-start = ((bf16[4,21,128,128]{2,3,1,0:T(8,128)(2,1)}), bf16[4,21,128,128]{2,3,1,0:T(8,128)(2,1)S(1)}, u32[]{:S(2)}, u32[]{:S(2)}) async-start(bf16[4,21,128,128]{2,3,1,0:T(8,128)(2,1)} %copy.51), calls=%async_computation | async-start | bytes 5505024 | tf_op jit(solution)/shard_map/all_to_all | solution.py:153
  21.5 93.0 %all-gather.3.cloned.1.call-start = ((), (), s32[]{:S(2)}) async-start(), calls=%async_computation.5 | async-start | bytes 4423680 | tf_op jit(solution)/shard_map/all_gather | solution.py:154
  61.7 28.1 %copy-start.5 = (s32[64]{0:T(128)}, s32[64]{0:T(128)S(1)}, u32[]{:S(2)}) copy-start(s32[64]{0:T(128)S(1)} %multiply_add_fusion) | copy-start | bytes 772
  62.5 38.0 %all-to-all-start.1 = ((s32[64,1,2]{2,1,0:T(1,128)}), s32[64,1,2]{2,1,0:T(1,128)S(1)}, u32[]{:S(2)}, u32[]{:S(2)}) async-start(s32[64,1,2]{2,1,0:T(1,128)} %bitcast.6), calls=%async_computation.1 | async-start | bytes 65536 | tf_op jit(solution)/shard_map/all_to_all | solution.py:186
  87.2 1.6 copy-start.2
  100.5 11.4 %copy-start.4 = (f32[3456]{0:T(1024)S(1)}, f32[3456]{0:T(1024)}, u32[]{:S(2)}) copy-start(f32[3456]{0:T(1024)} %param.20) | copy-start | bytes 41476
  100.6 106.5 %all-to-all-start.2 = ((bf16[64,2,128,128]{3,2,1,0:T(8,128)(2,1)}), bf16[64,2,128,128]{3,2,1,0:T(8,128)(2,1)}, u32[]{:S(2)}, u32[]{:S(2)}) async-start(bf16[64,2,128,128]{3,2,1,0:T(8,128)(2,1)} %bitcast.55), calls=%async_computation.2 | async-start | bytes 8388608 | tf_op jit(solution)/shard_map/all_to_all | solution.py:182
  111.2 46.6 %all-gather.5.cloned.1.call-start = ((), (), s32[]{:S(2)}) async-start(), calls=%async_computation.6 | async-start | bytes 4423680 | tf_op jit(solution)/shard_map/all_gather | solution.py:155
  233.3 102.1 %copy-start.6 = (s32[64]{0:T(128)S(1)}, s32[64]{0:T(128)}, u32[]{:S(2)}) copy-start(s32[64]{0:T(128)} %copy-done.5) | copy-start | bytes 772
  341.7 29.8 %copy-start.1 = (bf16[64,128,128]{2,1,0:T(8,128)(2,1)S(1)}, bf16[64,128,128]{2,1,0:T(8,128)(2,1)}, u32[]{:S(2)}) copy-start(bf16[64,128,128]{2,1,0:T(8,128)(2,1)} %copy-done) | copy-start | bytes 6291460
  374.1 5.7 %copy-start.7 = (s32[64]{0:T(128)S(1)}, s32[64]{0:T(128)}, u32[]{:S(2)}) copy-start(s32[64]{0:T(128)} %param.14) | copy-start | bytes 772
Sparse Core Ops, SparseCore 0:
  24.1 60.0 all-gather.2
  113.9 43.9 all-gather.4

commit v4 on v3

--- a/solution.py
+++ b/solution.py
@@ -7,6 +7,7 @@
 
 FEATURES = 26
 DEPTH = 2
+SLOT_ROWS = 8
 SAMPLE_BLOCKS = 2
 BAG_BLOCKS = 52
 
@@ -15,7 +16,7 @@
     slot_ref, arrived_ref, dense_ref, v_ref, u_ref, bias_ref, cot_ref,
     out_ref, ret_ref, pooled_ref, layer_ref, dscale_ref, dlayer_ref, bag_ref,
 ):
-    entries, block_size, emb_width = arrived_ref.shape
+    entries, block_size, emb_width = ret_ref.shape
     bags = pooled_ref.shape[0]
     chunks = layer_ref.shape[1] // emb_width
     f32, bf16 = jnp.float32, jnp.bfloat16
@@ -27,7 +28,8 @@
 
         @pl.when(slot >= 0)
         def _():
-            pooled_ref[slot] += arrived_ref[i].astype(f32)
+            rows = pl.ds(pl.multiple_of((i % DEPTH) * block_size, block_size), block_size)
+            pooled_ref[slot] += arrived_ref[i // DEPTH, rows, :].astype(f32)
 
         return carry
 
@@ -80,9 +82,9 @@
 
 
 def owner_work(arrived, arrived_slot, dense, cross_v, cross_u, cross_bias, cotangent):
-    block_size = arrived.shape[-2]
     emb_width = arrived.shape[-1]
-    entries = arrived.shape[0] * arrived.shape[1]
+    block_size = emb_width
+    entries = arrived.shape[0] * DEPTH
     samples, width = cotangent.shape
     rank = cross_v.shape[1]
     vmem = pl.BlockSpec(memory_space=pltpu.VMEM)
@@ -107,14 +109,14 @@
         cost_estimate=pl.CostEstimate(flops=flops, bytes_accessed=nbytes, transcendentals=0),
     )(
         arrived_slot.reshape(-1),
-        arrived.reshape(entries, block_size, emb_width),
+        arrived,
         dense,
         cross_v,
         cross_u,
         cross_bias.reshape(1, -1),
         cotangent,
     )
-    return cross_out, returning.reshape(arrived.shape)
+    return cross_out, returning.reshape(-1, DEPTH, block_size, emb_width)
 
 
 def body(
@@ -151,6 +153,7 @@
         axis=1,
     )
     incoming = lax.all_to_all(outgoing, "node", split_axis=0, concat_axis=0, tiled=True)
+    cross_v, cross_u, incoming = lax.optimization_barrier((cross_v, cross_u, incoming))
     full_v = lax.all_gather(cross_v, "node", axis=0, tiled=True)
     full_u = lax.all_gather(cross_u, "node", axis=0, tiled=True)
     moved_mult = incoming[:, :per_node].reshape(tile_count, block_size, block_size)
@@ -179,13 +182,13 @@
     ).astype(jnp.bfloat16)
     send_slot = jnp.max(jnp.where(chosen, moved_slot[None, :], -1), axis=1)
 
-    arrived = lax.all_to_all(
-        send_rows.reshape(tables, DEPTH, block_size, emb_width),
-        "table", split_axis=0, concat_axis=0, tiled=True,
-    )
-    arrived_slot = lax.all_to_all(
-        send_slot.reshape(tables, DEPTH), "table", split_axis=0, concat_axis=0, tiled=True
-    )
+    slot_rows = jnp.zeros((tables, SLOT_ROWS, emb_width), jnp.bfloat16)
+    slot_rows = slot_rows.at[:, 0, :DEPTH].set(send_slot.reshape(tables, DEPTH).astype(jnp.bfloat16))
+    outgoing = jnp.concatenate(
+        [send_rows.reshape(tables, DEPTH * block_size, emb_width), slot_rows], axis=1
+    )
+    arrived = lax.all_to_all(outgoing, "table", split_axis=0, concat_axis=0, tiled=True)
+    arrived_slot = arrived[:, DEPTH * block_size, :DEPTH].astype(jnp.int32)
     cross_out, returning = owner_work(
         arrived, arrived_slot, dense, full_v, full_u, cross_bias, cotangent
     )

time: 394 us -> 392 us (level)
  blocking collectives: 132 us -> 168 us
  waiting for transfers between devices: 132 us -> 97.9 us
  starting transfers between devices: 36 us -> 15.3 us
  local copies, waits for them, and re-layouts: 26.9 us -> 35.7 us
  other arithmetic: 6.11 us -> 11.2 us
    all_gather x1, waiting for transfers between devices: 43.4 us -> 0.01 us  [body(): full_u = lax.all_gather(cross_u, 'node', axis=0, tiled=True)]
    all_to_all x0 -> x1, blocking collectives: none -> 35.9 us  [body(): lax.all_to_all(outgoing, 'node', split_axis=0, concat_axis=0, tiled=True)]
    all_to_all x3 -> x1, starting transfers between devices: 35.8 us -> 15.1 us  [body(): lax.all_to_all(outgoing, 'table', split_axis=0, concat_axis=0, tiled=True)]
    all_to_all x3 -> x1, waiting for transfers between devices: 87.6 us -> 97.3 us  [body(): lax.all_to_all(outgoing, 'table', split_axis=0, concat_axis=0, tiled=True)]
    reshape x1, local copies, waits for them, and re-layouts: 0.65 us -> 7.46 us  [body(): send_rows.reshape(tables, DEPTH * block_size, emb_width)]
    optimization_barrier x0 -> x2, local copies, waits for them, and re-layouts: none -> 6.69 us  [body(): lax.optimization_barrier((cross_v, cross_u, incoming))]
    unnamed x19 -> x15, local copies, waits for them, and re-layouts: 7.66 us -> 3.11 us
    concatenate x0 -> x1, other arithmetic: none -> 3.94 us  [body(): jnp.concatenate([send_rows.reshape(tables, DEPTH * block_size, emb_width)...]
  transfers between devices with their start and end apart: 5 -> 3, of which waited for: 3 -> 1; matrix products, arithmetic and copies ran while one was open for 5% -> 7% of each run, Pallas kernels for 0% -> 0%
where the time goes in v4:
time: 392 us; the launch traced here: 391 us
  blocking collectives  168 us (43%)
  waiting for transfers between devices  97.9 us (25%)
  local copies, waits for them, and re-layouts  35.7 us (9%)
  Pallas kernels  26.8 us (7%)
  matrix products  22.4 us (6%)
  starting transfers between devices  15.3 us (4%)
  between operations  14.2 us (4%)
  other arithmetic  11.2 us (3%)
    all_to_all x1, blocking collectives, body(): lax.all_to_all(returning, 'table', split_axis=0, concat_axis=0, tiled=True)  102 us
    all_to_all x1, waiting for transfers between devices, body(): lax.all_to_all(outgoing, 'table', split_axis=0, concat_axis=0, tiled=True)  97.3 us
    all_to_all x1, blocking collectives, body(): lax.all_to_all(outgoing, 'node', split_axis=0, concat_axis=0, tiled=True)  35.9 us
    all_to_all x1, blocking collectives, body(): lax.all_to_all(tile_grad.reshape(tile_count, block_size, emb_width), 'nod...  29.6 us
    pallas_call x1, Pallas kernels, owner_work(): pl.pallas_call(cross_kernel, out_shape=(jax.ShapeDtypeStruct((samples, wi...  26.8 us
    all_to_all x1, starting transfers between devices, body(): lax.all_to_all(outgoing, 'table', split_axis=0, concat_axis=0, tiled=True)  15.1 us
    dot_general x1, matrix products, body(): jnp.dot(chosen.astype(jnp.float32), products, precision=lax.Precision.HIG...  8.81 us
  transfers between devices with their start and end apart: 3, of which 1 were waited for; matrix products, arithmetic and copies ran while one was open for 7% of the time, Pallas kernels for 0%

profile of v4, /device:TPU:1, one launch (start us, length us, event | category | flops | bytes accessed | tf_op | source)
XLA Modules:
  0.0 391.1 jit_solution(2880247668923545593)
XLA Ops:
  7.2 0.0 copy-start.2
  7.2 0.0 all-gather.3.cloned.1.call-start
  7.2 0.7 convert.14
  7.9 0.1 stack.12
  8.0 0.7 convert.15
  8.7 0.1 stack.13
  8.7 0.7 convert.16
  9.4 0.1 stack.14
  9.5 0.1 copy.47
  9.6 2.7 convert_element_type.52
  12.3 0.0 copy-start
  12.3 0.0 copy-done.2
  12.3 0.1 broadcast_in_dim.56
  12.4 1.2 copy-done
  13.6 0.4 fusion.10
  14.0 2.7 copy.48
  16.7 35.9 %all_to_all.20 = bf16[4,21,128,128]{2,3,1,0:T(8,128)(2,1)S(1)} all-to-all(bf16[4,21,128,128]{2,3,1,0:T(8,128)(2,1)} %copy.48), channel_id=1, replica_groups=mesh['node'=4,'table'=64] {'node'}, dimensions={0} | all-to-all | bytes 5505024 | tf_op jit(solution)/shard_map/all_to_all | solution.py:155
  52.6 2.7 copy.50
  55.2 4.0 %copy.49 = bf16[4,21,128,128]{2,0,3,1:T(4,128)(2,1)} copy(bf16[4,21,128,128]{2,3,1,0:T(8,128)(2,1)S(1)} %all_to_all.20) | data formatting | bytes 5505024 | tf_op jit(solution)/shard_map/optimization_barrier | solution.py:156
  59.3 0.0 slice-start
  59.3 0.0 slice-start.1
  59.3 0.0 all-gather.3.cloned.1.call-update
  59.3 0.8 slice_convert_fusion.1
  60.1 0.1 reshape.275
  60.2 0.2 select_reduce_fusion.1
  60.4 0.8 gather_fusion
  61.2 0.0 copy-start.4
  61.2 0.1 select_reduce_fusion
  61.3 0.2 convert_element_type.64
  61.5 0.0 slice-done
  61.6 2.2 gather_fusion.1
  63.7 0.0 slice-done.1
  63.7 2.4 fusion.11
  66.1 0.0 copy-done.4
  66.1 8.8 %convolution_convert_fusion = bf16[128,16384]{1,0:T(8,128)(2,1)} fusion(f32[8,8,128,128]{3,2,1,0:T(8,128)S(1)} %bitcast.46, s32[64]{0:T(128)S(1)} %multiply_add_fusion), kind=kOutput, calls=%fused_computation.2 | convolution fusion | flops 1612718080 | bytes 8388864 | tf_op jit(solution)/shard_map/dot_general | solution.py:179
  75.0 7.5 %reshape.268 = bf16[64,256,128]{2,1,0:T(8,128)(2,1)} reshape(bf16[128,16384]{1,0:T(8,128)(2,1)} %convolution_convert_fusion) | data formatting | bytes 8388608 | tf_op jit(solution)/shard_map/reshape | solution.py:188
  82.4 3.9 %fusion.2 = bf16[64,264,128]{2,1,0:T(8,128)(2,1)} fusion(bf16[64,1,2]{2,1,0:T(2,128)(2,1)S(1)} %convert_element_type.64, bf16[64,256,128]{2,1,0:T(8,128)(2,1)} %reshape.268), kind=kLoop, calls=%fused_computation.8 | loop fusion | flops 12976128 | bytes 8519936 | tf_op jit(solution)/shard_map/concatenate | solution.py:187
  86.4 0.0 copy-start.3
  86.4 15.1 %all-to-all-start.1 = ((bf16[64,264,128]{2,1,0:T(8,128)(2,1)}), bf16[64,264,128]{2,1,0:T(8,128)(2,1)}, u32[]{:S(2)}, u32[]{:S(2)}) async-start(bf16[64,264,128]{2,1,0:T(8,128)(2,1)} %fusion.2), calls=%async_computation.1 | async-start | bytes 8650752 | tf_op jit(solution)/shard_map/all_to_all | solution.py:190
  101.4 0.2 all-gather.5.cloned.1.call-start
  101.6 0.5 all-gather.5.cloned.1.call-update
  102.2 0.0 copy-done.3
  102.2 0.6 reshape.269.bias_ref
  102.8 97.3 %all-to-all-done.1.arrived_ref = bf16[64,264,128]{2,1,0:T(8,128)(2,1)} async-done(((bf16[64,264,128]{2,1,0:T(8,128)(2,1)}), bf16[64,264,128]{2,1,0:T(8,128)(2,1)}, u32[]{:S(2)}, u32[]{:S(2)}) %all-to-all-start.1) | async-done | bytes 4325408 | tf_op jit(solution)/shard_map/all_to_all | solution.py:190
  200.1 1.0 fusion.18
  201.2 0.7 reshape.276.slot_ref
  201.9 0.0 all-gather.3.cloned.1.call-done.v_ref
  201.9 0.0 all-gather.5.cloned.1.call-done.u_ref
  201.9 26.8 %shard_map.113 = (bf16[256,3456]{1,0:T(8,128)(2,1)}, bf16[128,128,128]{2,1,0:T(8,128)(2,1)}) custom-call(s32[128]{0:T(128)} %reshape.276.slot_ref, bf16[64,264,128]{2,1,0:T(8,128)(2,1)} %all-to-all-done.1.arrived_ref, bf16[256,128]{1,0:T(8,128)(2,1)} %dense_ref.1, bf16[3456,512]{1,0:T(8,128)(2,1)} %all-gather.3.cloned.1.call-done.v_ref, ...), custom_call_target="tpu_custom_call" | custom-call | flops 3623878656 | bytes 19005440 | tf_op jit(solution)/shard_map/pallas_call | solution.py:93
  228.7 0.0 copy-start.5
  228.7 102.1 %all_to_all.21 = bf16[64,2,128,128]{3,2,1,0:T(8,128)(2,1)S(1)} all-to-all(bf16[64,2,128,128]{3,2,1,0:T(8,128)(2,1)} %bitcast.52), channel_id=1, replica_groups=mesh['node'=4,'table'=64] {'table'}, dimensions={0} | all-to-all | bytes 8388608 | tf_op jit(solution)/shard_map/all_to_all | solution.py:195
  330.8 0.0 copy-done.5
  330.8 2.8 fusion.14
  333.6 1.9 copy.57
  335.5 0.0 copy-start.1
  335.5 4.2 %copy.53 = bf16[64,128,128]{1,2,0:T(8,128)(2,1)} copy(bf16[64,128,128]{2,1,0:T(8,128)(2,1)} %bitcast.51) | data formatting | bytes 4194304 | tf_op jit(solution)/shard_map/reshape | solution.py:201
  339.7 29.6 %all_to_all.22 = bf16[64,128,128]{1,2,0:T(8,128)(2,1)S(1)} all-to-all(bf16[64,128,128]{1,2,0:T(8,128)(2,1)} %copy.53), channel_id=1, replica_groups=mesh['node'=4,'table'=64] {'node'}, dimensions={0} | all-to-all | bytes 4194304 | tf_op jit(solution)/shard_map/all_to_all | solution.py:200
  369.3 0.0 copy-done.1
  369.3 2.7 convolution_bitcast_fusion
  372.0 0.0 copy-start.6
  372.0 5.6 %copy.54 = f32[64,128,128]{2,1,0:T(8,128)} copy(f32[64,128,128]{1,2,0:T(8,128)} %convolution_bitcast_fusion) | data formatting | bytes 8388608 | tf_op jit(solution)/shard_map/kbr,kbe->kre/dot_general | solution.py:204
  377.6 0.0 copy-done.6
  377.6 5.8 %fusion.3 = f32[4,16384]{1,0:T(4,128)S(1)} fusion(f32[8,8,128,128]{3,2,1,0:T(8,128)} %bitcast.48, s32[64]{0:T(128)S(1)} %copy-done.6), kind=kOutput, calls=%fused_computation.9 | convolution fusion | flops 50331904 | bytes 4456704 | tf_op jit(solution)/shard_map/dot_general | solution.py:210
  383.4 0.9 reshape.274
  (8 shorter events, 0.1 us)
Async XLA Ops:
  7.2 5.1 %copy-start.2 = (bf16[512,128]{1,0:T(8,128)(2,1)S(1)}, bf16[512,128]{1,0:T(8,128)(2,1)}, u32[]{:S(2)}) copy-start(bf16[512,128]{1,0:T(8,128)(2,1)} %param.14) | copy-start | bytes 393220
  7.2 194.7 %all-gather.3.cloned.1.call-start = ((), (), s32[]{:S(2)}) async-start(), calls=%async_computation.4 | async-start | bytes 4423680 | tf_op jit(solution)/shard_map/all_gather | solution.py:157
  12.3 1.3 copy-start
  59.3 2.3 slice-start
  59.3 4.5 %slice-start.1 = ((bf16[4,21,128,128]{3,2,1,0:T(8,128)(2,1)}), bf16[4,16,128,128]{3,2,1,0:T(8,128)(2,1)S(1)}, s32[]{:S(2)}) async-start(bf16[4,21,128,128]{3,2,1,0:T(8,128)(2,1)} %copy.50), calls=%async_computation.7 | async-start | bytes 4194304 | tf_op jit(solution)/shard_map/slice | solution.py:159
  61.2 4.9 %copy-start.4 = (s32[64]{0:T(128)}, s32[64]{0:T(128)S(1)}, u32[]{:S(2)}) copy-start(s32[64]{0:T(128)S(1)} %multiply_add_fusion) | copy-start | bytes 772
  86.4 15.8 %copy-start.3 = (f32[3456]{0:T(1024)S(1)}, f32[3456]{0:T(1024)}, u32[]{:S(2)}) copy-start(f32[3456]{0:T(1024)} %param.22) | copy-start | bytes 41476
  86.4 113.8 %all-to-all-start.1 = ((bf16[64,264,128]{2,1,0:T(8,128)(2,1)}), bf16[64,264,128]{2,1,0:T(8,128)(2,1)}, u32[]{:S(2)}, u32[]{:S(2)}) async-start(bf16[64,264,128]{2,1,0:T(8,128)(2,1)} %fusion.2), calls=%async_computation.1 | async-start | bytes 8650752 | tf_op jit(solution)/shard_map/all_to_all | solution.py:190
  101.4 100.5 %all-gather.5.cloned.1.call-start = ((), (), s32[]{:S(2)}) async-start(), calls=%async_computation.5 | async-start | bytes 4423680 | tf_op jit(solution)/shard_map/all_gather | solution.py:158
  228.7 102.1 %copy-start.5 = (s32[64]{0:T(128)S(1)}, s32[64]{0:T(128)}, u32[]{:S(2)}) copy-start(s32[64]{0:T(128)} %copy-done.4) | copy-start | bytes 772
  335.5 33.8 %copy-start.1 = (bf16[64,128,128]{2,1,0:T(8,128)(2,1)S(1)}, bf16[64,128,128]{2,1,0:T(8,128)(2,1)}, u32[]{:S(2)}) copy-start(bf16[64,128,128]{2,1,0:T(8,128)(2,1)} %copy-done) | copy-start | bytes 6291460
  372.0 5.6 %copy-start.6 = (s32[64]{0:T(128)S(1)}, s32[64]{0:T(128)}, u32[]{:S(2)}) copy-start(s32[64]{0:T(128)} %param.16) | copy-start | bytes 772
Sparse Core Ops, SparseCore 0:
  59.4 49.0 all-gather.2
  110.3 45.6 all-gather.4

commit v5 on v4

--- a/solution.py
+++ b/solution.py
@@ -10,6 +10,47 @@
 SLOT_ROWS = 8
 SAMPLE_BLOCKS = 2
 BAG_BLOCKS = 52
+
+
+def combine_kernel(entry_ref, row_ref, incoming_ref, slots_ref, out_ref, acc_ref):
+    tiles = entry_ref.shape[0]
+    nodes, _, block_size, emb_width = incoming_ref.shape
+    per_node = tiles // nodes
+    entries = acc_ref.shape[0]
+    acc_ref[...] = jnp.zeros_like(acc_ref)
+
+    def add_tile(k, carry):
+        source = k // per_node
+        block = row_ref[k]
+        product = jnp.dot(
+            incoming_ref[source, k % per_node],
+            incoming_ref[source, per_node + block],
+            preferred_element_type=jnp.float32,
+        )
+        acc_ref[entry_ref[k]] += product
+        return carry
+
+    lax.fori_loop(0, tiles, add_tile, 0)
+
+    def store(i, carry):
+        rows = pl.ds(pl.multiple_of((i % DEPTH) * block_size, block_size), block_size)
+        out_ref[i // DEPTH, rows, :] = acc_ref[i].astype(jnp.bfloat16)
+        return carry
+
+    lax.fori_loop(0, entries, store, 0)
+    out_ref[:, DEPTH * block_size:, :] = slots_ref[...]
+
+
+def grad_kernel(row_ref, mult_ref, grad_ref, out_ref):
+    out_ref[...] = jnp.zeros_like(out_ref)
+
+    def add_tile(k, carry):
+        out_ref[row_ref[k]] += lax.dot_general(
+            mult_ref[k], grad_ref[k], (((0,), (0,)), ((), ())), preferred_element_type=jnp.float32
+        )
+        return carry
+
+    lax.fori_loop(0, mult_ref.shape[0], add_tile, 0)
 
 
 def cross_kernel(
@@ -156,19 +197,10 @@
     cross_v, cross_u, incoming = lax.optimization_barrier((cross_v, cross_u, incoming))
     full_v = lax.all_gather(cross_v, "node", axis=0, tiled=True)
     full_u = lax.all_gather(cross_u, "node", axis=0, tiled=True)
-    moved_mult = incoming[:, :per_node].reshape(tile_count, block_size, block_size)
-    peer_rows = incoming[:, per_node:per_node + local_blocks].reshape(-1, block_size, emb_width)
     moved_meta = incoming[:, -1, :per_node, :3].reshape(tile_count, 3).astype(jnp.int32)
-
     moved_table = moved_meta[:, 0]
     moved_slot = moved_meta[:, 1]
     sequence = jnp.arange(tile_count, dtype=jnp.int32)
-    source = sequence // per_node
-    moved_rows = source * local_blocks + moved_meta[:, 2]
-    picked = jnp.take(peer_rows, moved_rows, axis=0)
-    products = jnp.einsum(
-        "kbr,kre->kbe", moved_mult, picked, preferred_element_type=jnp.float32
-    ).reshape(tile_count, -1)
 
     same_table = moved_table[:, None] == moved_table[None, :]
     first = jnp.min(jnp.where(same_table, sequence[None, :], tile_count), axis=1)
@@ -176,17 +208,27 @@
     entry = moved_table * DEPTH + (moved_slot != first_slot).astype(jnp.int32)
     entries = tables * DEPTH
     chosen = entry[None, :] == jnp.arange(entries, dtype=jnp.int32)[:, None]
-    send_rows = jnp.dot(
-        chosen.astype(jnp.float32), products, precision=lax.Precision.HIGHEST,
-        preferred_element_type=jnp.float32,
-    ).astype(jnp.bfloat16)
     send_slot = jnp.max(jnp.where(chosen, moved_slot[None, :], -1), axis=1)
 
     slot_rows = jnp.zeros((tables, SLOT_ROWS, emb_width), jnp.bfloat16)
     slot_rows = slot_rows.at[:, 0, :DEPTH].set(send_slot.reshape(tables, DEPTH).astype(jnp.bfloat16))
-    outgoing = jnp.concatenate(
-        [send_rows.reshape(tables, DEPTH * block_size, emb_width), slot_rows], axis=1
-    )
+    vmem = pl.BlockSpec(memory_space=pltpu.VMEM)
+    smem = pl.BlockSpec(memory_space=pltpu.SMEM)
+    outgoing = pl.pallas_call(
+        combine_kernel,
+        out_shape=jax.ShapeDtypeStruct(
+            (tables, DEPTH * block_size + SLOT_ROWS, emb_width), jnp.bfloat16
+        ),
+        in_specs=[smem, smem, vmem, vmem],
+        out_specs=vmem,
+        scratch_shapes=[pltpu.VMEM((entries, block_size, emb_width), jnp.float32)],
+        compiler_params=pltpu.CompilerParams(vmem_limit_bytes=48 * 1024 * 1024),
+        cost_estimate=pl.CostEstimate(
+            flops=2 * tile_count * block_size ** 3,
+            bytes_accessed=2 * (incoming.size + entries * block_size * emb_width),
+            transcendentals=0,
+        ),
+    )(entry, moved_meta[:, 2], incoming, slot_rows)
     arrived = lax.all_to_all(outgoing, "table", split_axis=0, concat_axis=0, tiled=True)
     arrived_slot = arrived[:, DEPTH * block_size, :DEPTH].astype(jnp.int32)
     cross_out, returning = owner_work(
@@ -201,18 +243,17 @@
         tile_grad.reshape(tile_count, block_size, emb_width),
         "node", split_axis=0, concat_axis=0, tiled=True,
     )
-    tile_grads = jnp.einsum(
-        "kbr,kbe->kre", mult_bf, tile_grad, preferred_element_type=jnp.float32
-    )
-    owner_rows = (
-        tile_rows[None, :] == jnp.arange(local_blocks, dtype=jnp.int32)[:, None]
-    ).astype(jnp.float32)
-    emb_grad = jnp.dot(
-        owner_rows,
-        tile_grads.reshape(tile_count, -1),
-        precision=lax.Precision.HIGHEST,
-        preferred_element_type=jnp.float32,
-    )
+    emb_grad = pl.pallas_call(
+        grad_kernel,
+        out_shape=jax.ShapeDtypeStruct((local_blocks, block_size, emb_width), jnp.float32),
+        in_specs=[smem, vmem, vmem],
+        out_specs=vmem,
+        cost_estimate=pl.CostEstimate(
+            flops=2 * tile_count * block_size ** 3,
+            bytes_accessed=2 * (mult_bf.size + tile_grad.size),
+            transcendentals=0,
+        ),
+    )(tile_rows, mult_bf, tile_grad)
     return (cross_out, emb_grad.reshape(-1, emb_width))
 
 

time: 392 us -> 364 us (0.929)
  local copies, waits for them, and re-layouts: 35.7 us -> 4.77 us
  Pallas kernels: 26.8 us -> 55.1 us
  matrix products: 22.4 us -> 2.81 us
  other arithmetic: 11.2 us -> 6.47 us
    pallas_call x0 -> x2, Pallas kernels: none -> 28.3 us  [the longest x1 14.8 us: body(): pl.pallas_call(grad_kernel, out_shape=jax.ShapeDtypeStruct((local_blocks,...]
    dot_general x4 -> x0, matrix products: 19.6 us -> none  [the longest x1 8.81 us: body(): jnp.dot(chosen.astype(jnp.float32), products, precision=lax.Precision.HIG...]
    reshape x3 -> x0, local copies, waits for them, and re-layouts: 12.6 us -> none  [the longest x1 7.46 us: body(): send_rows.reshape(tables, DEPTH * block_size, emb_width)]
    optimization_barrier x2 -> x0, local copies, waits for them, and re-layouts: 6.69 us -> none  [body(): lax.optimization_barrier((cross_v, cross_u, incoming))]
    dot_general x1 -> x0, local copies, waits for them, and re-layouts: 5.64 us -> none  [body(): jnp.einsum('kbr,kbe->kre', mult_bf, tile_grad, preferred_element_type=jnp...]
    concatenate x1 -> x0, other arithmetic: 3.94 us -> none  [body(): jnp.concatenate([send_rows.reshape(tables, DEPTH * block_size, emb_width)...]
  transfers between devices with their start and end apart: 3 -> 3, of which waited for: 1 -> 1; matrix products, arithmetic and copies ran while one was open for 7% -> 1% of each run, Pallas kernels for 0% -> 4%
where the time goes in v5:
time: 364 us
  blocking collectives  168 us (46%)
  waiting for transfers between devices  98.1 us (27%)
  Pallas kernels  55.1 us (15%)
  between operations  14.2 us (4%)
  starting transfers between devices  14 us (4%)
  other arithmetic  6.47 us (2%)
  local copies, waits for them, and re-layouts  4.77 us (1%)
    all_to_all x1, blocking collectives, body(): lax.all_to_all(returning, 'table', split_axis=0, concat_axis=0, tiled=True)  102 us
    all_to_all x1, waiting for transfers between devices, body(): lax.all_to_all(outgoing, 'table', split_axis=0, concat_axis=0, tiled=True)  97.3 us
    all_to_all x1, blocking collectives, body(): lax.all_to_all(outgoing, 'node', split_axis=0, concat_axis=0, tiled=True)  36.9 us
    all_to_all x1, blocking collectives, body(): lax.all_to_all(tile_grad.reshape(tile_count, block_size, emb_width), 'nod...  29.3 us
    pallas_call x1, Pallas kernels, owner_work(): pl.pallas_call(cross_kernel, out_shape=(jax.ShapeDtypeStruct((samples, wi...  26.7 us
    pallas_call x1, Pallas kernels, body(): pl.pallas_call(grad_kernel, out_shape=jax.ShapeDtypeStruct((local_blocks,...  14.8 us
    all_to_all x1, starting transfers between devices, body(): lax.all_to_all(outgoing, 'table', split_axis=0, concat_axis=0, tiled=True)  14 us
    pallas_call x1, Pallas kernels, body(): pl.pallas_call(combine_kernel, out_shape=jax.ShapeDtypeStruct((tables, DE...  13.5 us
  transfers between devices with their start and end apart: 3, of which 1 were waited for; matrix products, arithmetic and copies ran while one was open for 1% of the time, Pallas kernels for 4%

profile of v5, /device:TPU:1, one launch (start us, length us, event | category | flops | bytes accessed | tf_op | source)
XLA Modules:
  0.0 363.7 jit_solution(15137552988175404469)
XLA Ops:
  7.2 0.0 copy-start.3
  7.2 0.0 all-gather.3.cloned.1.call-start
  7.2 0.7 convert.14
  7.9 0.1 stack.12
  8.0 0.7 convert.15
  8.7 0.1 stack.13
  8.7 0.7 convert.16
  9.4 0.1 stack.14
  9.5 0.1 copy.31
  9.6 2.7 convert_element_type.47.mult_ref
  12.3 0.0 copy-start.2
  12.3 0.0 copy-done.3
  12.3 0.1 broadcast_in_dim.44
  12.4 1.2 copy-done.2
  13.6 0.4 fusion.3
  14.0 36.9 %all_to_all.20.incoming_ref = bf16[4,21,128,128]{3,2,1,0:T(8,128)(2,1)S(1)} all-to-all(bf16[4,21,128,128]{3,2,1,0:T(8,128)(2,1)S(1)} %fusion.3), channel_id=1, replica_groups=mesh['node'=4,'table'=64] {'node'}, dimensions={0} | all-to-all | bytes 5505024 | tf_op jit(solution)/shard_map/all_to_all | solution.py:196
  50.9 0.0 all-gather.3.cloned.1.call-update
  51.0 0.1 fusion.10
  51.1 0.1 copy.38
  51.1 0.1 copy.37
  51.2 0.1 copy.36
  51.3 0.2 select_reduce_fusion.1
  51.5 0.8 gather_fusion
  52.3 0.0 copy-start
  52.3 0.1 select_reduce_fusion
  52.4 0.2 convert_element_type.58
  52.7 13.5 %shard_map.113 = bf16[64,264,128]{2,1,0:T(8,128)(2,1)} custom-call(s32[64]{0:T(128)S(1)} %multiply_add_fusion.entry_ref, s32[64]{0:T(128)S(1)} %bitcast.26, bf16[4,21,128,128]{3,2,1,0:T(8,128)(2,1)S(1)} %all_to_all.20.incoming_ref, bf16[64,8,128]{2,1,0:T(8,128)(2,1)S(1)} %scatter.9.slots_ref), custom_call_target="tpu_custom_call" | custom-call | flops 268435456 | bytes 6946816 | tf_op jit(solution)/shard_map/pallas_call | solution.py:217
  66.2 0.0 copy-done
  66.2 0.0 copy-start.4
  66.2 14.0 %all-to-all-start.1 = ((bf16[64,264,128]{2,1,0:T(8,128)(2,1)}), bf16[64,264,128]{2,1,0:T(8,128)(2,1)}, u32[]{:S(2)}, u32[]{:S(2)}) async-start(bf16[64,264,128]{2,1,0:T(8,128)(2,1)} %shard_map.113), calls=%async_computation.1 | async-start | bytes 8650752 | tf_op jit(solution)/shard_map/all_to_all | solution.py:232
  80.2 0.0 all-gather.5.cloned.1.call-start
  80.2 0.7 all-gather.5.cloned.1.call-update
  80.9 0.0 copy-done.4
  80.9 0.6 reshape.207.bias_ref
  81.5 97.3 %all-to-all-done.1.arrived_ref = bf16[64,264,128]{2,1,0:T(8,128)(2,1)} async-done(((bf16[64,264,128]{2,1,0:T(8,128)(2,1)}), bf16[64,264,128]{2,1,0:T(8,128)(2,1)}, u32[]{:S(2)}, u32[]{:S(2)}) %all-to-all-start.1) | async-done | bytes 4325408 | tf_op jit(solution)/shard_map/all_to_all | solution.py:232
  178.9 1.0 fusion.7
  179.9 0.6 reshape.213.slot_ref
  180.5 0.0 all-gather.3.cloned.1.call-done.v_ref
  180.5 0.0 all-gather.5.cloned.1.call-done.u_ref
  180.5 26.7 %shard_map.114 = (bf16[256,3456]{1,0:T(8,128)(2,1)}, bf16[128,128,128]{2,1,0:T(8,128)(2,1)}) custom-call(s32[128]{0:T(128)} %reshape.213.slot_ref, bf16[64,264,128]{2,1,0:T(8,128)(2,1)} %all-to-all-done.1.arrived_ref, bf16[256,128]{1,0:T(8,128)(2,1)} %dense_ref.1, bf16[3456,512]{1,0:T(8,128)(2,1)} %all-gather.3.cloned.1.call-done.v_ref, ...), custom_call_target="tpu_custom_call" | custom-call | flops 3623878656 | bytes 19005440 | tf_op jit(solution)/shard_map/pallas_call | solution.py:134
  207.3 0.0 copy-start.1
  207.3 102.1 %all_to_all.21 = bf16[64,2,128,128]{3,2,1,0:T(8,128)(2,1)S(1)} all-to-all(bf16[64,2,128,128]{3,2,1,0:T(8,128)(2,1)} %bitcast.32), channel_id=1, replica_groups=mesh['node'=4,'table'=64] {'table'}, dimensions={0} | all-to-all | bytes 8388608 | tf_op jit(solution)/shard_map/all_to_all | solution.py:237
  309.4 0.0 copy-done.1
  309.4 2.8 fusion.4
  312.2 0.6 copy.40
  312.8 29.3 %all_to_all.22.grad_ref = bf16[64,128,128]{2,1,0:T(8,128)(2,1)} all-to-all(bf16[64,128,128]{2,1,0:T(8,128)(2,1)S(1)} %bitcast.31), channel_id=1, replica_groups=mesh['node'=4,'table'=64] {'node'}, dimensions={0} | all-to-all | bytes 4194304 | tf_op jit(solution)/shard_map/all_to_all | solution.py:242
  342.1 14.8 %shard_map.115 = f32[4,128,128]{2,1,0:T(8,128)} custom-call(s32[64]{0:T(128)} %row_ref.1, bf16[64,128,128]{2,1,0:T(8,128)(2,1)} %copy-done.2, bf16[64,128,128]{2,1,0:T(8,128)(2,1)} %all_to_all.22.grad_ref), custom_call_target="tpu_custom_call" | custom-call | flops 268435456 | bytes 4194304 | tf_op jit(solution)/shard_map/pallas_call | solution.py:246
  (8 shorter events, 0.1 us)
Async XLA Ops:
  7.2 5.1 %copy-start.3 = (bf16[512,128]{1,0:T(8,128)(2,1)S(1)}, bf16[512,128]{1,0:T(8,128)(2,1)}, u32[]{:S(2)}) copy-start(bf16[512,128]{1,0:T(8,128)(2,1)} %param.14) | copy-start | bytes 393220
  7.2 173.4 %all-gather.3.cloned.1.call-start = ((), (), s32[]{:S(2)}) async-start(), calls=%async_computation.4 | async-start | bytes 4423680 | tf_op jit(solution)/shard_map/all_gather | solution.py:198
  12.3 1.3 copy-start.2
  52.3 13.9 %copy-start = (s32[64]{0:T(128)}, s32[64]{0:T(128)S(1)}, u32[]{:S(2)}) copy-start(s32[64]{0:T(128)S(1)} %multiply_add_fusion.entry_ref) | copy-start | bytes 772
  66.2 14.7 %copy-start.4 = (f32[3456]{0:T(1024)S(1)}, f32[3456]{0:T(1024)}, u32[]{:S(2)}) copy-start(f32[3456]{0:T(1024)} %param.22) | copy-start | bytes 41476
  66.2 112.7 %all-to-all-start.1 = ((bf16[64,264,128]{2,1,0:T(8,128)(2,1)}), bf16[64,264,128]{2,1,0:T(8,128)(2,1)}, u32[]{:S(2)}, u32[]{:S(2)}) async-start(bf16[64,264,128]{2,1,0:T(8,128)(2,1)} %shard_map.113), calls=%async_computation.1 | async-start | bytes 8650752 | tf_op jit(solution)/shard_map/all_to_all | solution.py:232
  80.2 100.4 %all-gather.5.cloned.1.call-start = ((), (), s32[]{:S(2)}) async-start(), calls=%async_computation.5 | async-start | bytes 4423680 | tf_op jit(solution)/shard_map/all_gather | solution.py:199
  207.3 102.1 %copy-start.1 = (s32[64]{0:T(128)S(1)}, s32[64]{0:T(128)}, u32[]{:S(2)}) copy-start(s32[64]{0:T(128)} %copy-done) | copy-start | bytes 772
Sparse Core Ops, SparseCore 0:
  51.1 47.8 all-gather.2
  100.8 45.6 all-gather.4
